TPU v7x, 128 devices: a whole 4x4x4 slice. The times are simulated.
128 devices in a mesh: layer: 64 (over z, y, x_hi, core), rows: 2 (over x_lo).
Axes of the slice: x: 4 (x_hi: 2, x_lo: 2; x = x_hi * 2 + x_lo), y: 4, z: 4, core: 2. Of those that a mesh axis runs over, the one named last changes fastest.
Arguments:
- state_guess: bfloat16 [64, 1, 16, 64, 256], P('layer', None, 'rows'), may hold values from -6 to 6
- adjoint_guess: bfloat16 [64, 1, 16, 64, 256], P('layer', None, 'rows'), may hold values from -6 to 6
- weights: bfloat16 [128, 9, 256, 256], P('layer'), may hold values from -0.125 to 0.125
- net_input: bfloat16 [1, 16, 64, 256], P(None, 'rows'), may hold values from -6 to 6
- final_cotangent: bfloat16 [1, 16, 64, 256], P(None, 'rows'), may hold values from -6 to 6
Outputs:
- states: bfloat16 [64, 1, 16, 64, 256], P('layer', None, 'rows')
- adjoints: bfloat16 [64, 1, 16, 64, 256], P('layer', None, 'rows')
- weight_grad: float32 [128, 9, 256, 256], P('layer', None, None, 'rows')
All inputs are finite; a program needn't handle non-finite values.
Results may differ from a plain program's by a relative error of at most 0.012.
Values may be sent and summed in bfloat16 or wider, within the bound.
A program may use at most 64 MiB of HBM per device.

v0:
```python
import math

import jax
import jax.numpy as jnp
from jax import lax
from jax.sharding import PartitionSpec as P


def with_halo(cells, sides, width):
    for axis, dim in sides:
        count = lax.axis_size(axis)
        ends = count - 1
        head = lax.slice_in_dim(cells, 0, width, axis=dim)
        tail = lax.slice_in_dim(cells, cells.shape[dim] - width, cells.shape[dim], axis=dim)
        cells = jnp.concatenate(
            [
                lax.ppermute(tail, axis, [(i, (i + 1) % count) for i in range(ends)]),
                cells,
                lax.ppermute(head, axis, [((i + 1) % count, i) for i in range(ends)]),
            ],
            axis=dim,
        )
    return cells


def passed_along(value, axis, steps):
    count = lax.axis_size(axis)
    initial, last = (max(0, -steps), min(count, count - steps))
    return lax.ppermute(value, axis, [(source, source + steps) for source in range(initial, last)])


def pad_cols(values):
    return jnp.pad(values, ((0, 0), (0, 0), (1, 1), (0, 0)))


def convolve(padded, kernel):
    widened = pad_cols(padded)
    row_count = padded.shape[1] - 2
    col_count = padded.shape[2]
    channels = kernel.shape[-1]
    summed = jnp.zeros((padded.shape[0] * row_count * col_count, channels), jnp.float32)
    for tap_row in range(3):
        for tap_col in range(3):
            window = widened[
                :, tap_row : tap_row + row_count, tap_col : tap_col + col_count, :
            ].reshape(-1, channels)
            summed = summed + jnp.dot(
                window, kernel[tap_row * 3 + tap_col], preferred_element_type=jnp.float32
            )
    return summed.reshape(padded.shape[0], row_count, col_count, channels)


def convolve_back(padded, kernel):
    widened = pad_cols(padded)
    row_count = padded.shape[1] - 2
    col_count = padded.shape[2]
    channels = kernel.shape[-1]
    summed = jnp.zeros((padded.shape[0] * row_count * col_count, channels), jnp.float32)
    for tap_row in range(3):
        for tap_col in range(3):
            window = widened[
                :, 2 - tap_row : 2 - tap_row + row_count, 2 - tap_col : 2 - tap_col + col_count, :
            ].reshape(-1, channels)
            summed = summed + lax.dot_general(
                window,
                kernel[tap_row * 3 + tap_col],
                (((1,), (1,)), ((), ())),
                preferred_element_type=jnp.float32,
            )
    return summed.reshape(padded.shape[0], row_count, col_count, channels)


def weight_term(padded, delta):
    widened = pad_cols(padded)
    row_count = delta.shape[1]
    col_count = delta.shape[2]
    channels = delta.shape[3]
    flat_delta = delta.reshape(-1, channels)
    taps = []
    for tap_row in range(3):
        for tap_col in range(3):
            window = widened[
                :, tap_row : tap_row + row_count, tap_col : tap_col + col_count, :
            ].reshape(-1, channels)
            taps.append(
                lax.dot_general(
                    window, flat_delta, (((0,), (0,)), ((), ())), preferred_element_type=jnp.float32
                )
            )
    return jnp.stack(taps)


def activation_slope(values):
    sigmoid_value = jax.nn.sigmoid(values)
    return sigmoid_value * (1.0 + values * (1.0 - sigmoid_value))


def advance(state, padded, kernel):
    pre_act = convolve(padded, kernel)
    return ((state.astype(jnp.float32) + 0.5 * jax.nn.silu(pre_act)).astype(jnp.bfloat16), pre_act)


def block_forward(padded, weights):
    middle, pre_first = advance(padded[:, 1:-1], padded, weights[0])
    middle_pad = with_halo(middle, (("rows", 1),), 1)
    block_end, pre_second = advance(middle, middle_pad, weights[1])
    return (middle, pre_first, block_end, pre_second, middle_pad)


def delta_halo(values):
    return with_halo(values, (("rows", 1),), 1)


def local(state_guess, adjoint_guess, weights, net_input, final_cotangent):
    rim_depth = 1
    is_first = lax.axis_index("layer") == 0
    is_last = lax.axis_index("layer") == lax.axis_size("layer") - 1
    band_rows = net_input.shape[1]
    height = band_rows * lax.axis_size("rows")
    start_state = state_guess[0]
    for sweep_index in range(3):
        padded = with_halo(start_state, (("rows", 1),), rim_depth)
        middle, pre_first, block_end, pre_second, middle_pad = block_forward(padded, weights)
        if sweep_index < 2:
            arrived = passed_along(block_end, "layer", 1)
            start_state = jnp.where(is_first, net_input, arrived)
    arrived_adjoint = passed_along(adjoint_guess[0], "layer", -1)
    end_float = jnp.where(is_last, final_cotangent, arrived_adjoint).astype(jnp.float32)
    delta_second = (0.5 * activation_slope(pre_second) * end_float).astype(jnp.bfloat16)
    back_middle = (end_float + convolve_back(delta_halo(delta_second), weights[1])).astype(
        jnp.bfloat16
    )
    delta_first = (0.5 * activation_slope(pre_first) * back_middle.astype(jnp.float32)).astype(
        jnp.bfloat16
    )
    adjoint = (
        back_middle.astype(jnp.float32) + convolve_back(delta_halo(delta_first), weights[0])
    ).astype(jnp.bfloat16)
    grad_scale = 1.0 / math.sqrt(net_input.shape[0] * height * net_input.shape[2])
    partial_value = (
        jnp.stack([weight_term(padded, delta_first), weight_term(middle_pad, delta_second)])
        * grad_scale
    )
    grads = lax.psum_scatter(
        partial_value.astype(jnp.bfloat16), "rows", scatter_dimension=3, tiled=True
    ).astype(jnp.float32)
    return (start_state[None], adjoint[None], grads)


def solution(mesh):
    in_specs = (
        P("layer", None, "rows", None, None),
        P("layer", None, "rows", None, None),
        P("layer", None, None, None),
        P(None, "rows", None, None),
        P(None, "rows", None, None),
    )
    out_specs = (
        P("layer", None, "rows", None, None),
        P("layer", None, "rows", None, None),
        P("layer", None, None, "rows"),
    )
    return jax.shard_map(local, mesh=mesh, in_specs=in_specs, out_specs=out_specs, check_vma=False)
```

profile of v0, /device:TPU:97, one launch (start us, length us, event | category | flops | bytes accessed | tf_op | source)
XLA Modules:
  0.0 180.3 jit_solution(2362695580732063651)
XLA Ops:
  9.4 4.0 %collective-permute-start = (bf16[1,1,64,256]{3,2,1,0:T(8,128)(2,1)S(1)}, bf16[1,1,64,256]{3,2,1,0:T(8,128)(2,1)S(1)}, u32[]{:S(2)}, u32[]{:S(2)}) collective-permute-start(bf16[1,1,64,256]{3,2,1,0:T(8,128)(2,1)S(1)} %get-tuple-element.83), channel_id=1, source_target_pairs={{0,1},{2,3},{4,5},{6,7},{8,9},{10,11},{12,13},{14,15},{16,17},{18,... | collective-permute-start | bytes 98312 | tf_op jit(solution)/shard_map/ppermute | solution.py:17
  18.3 1.3 collective-permute-start.3
  19.6 4.0 %collective-permute-start.2 = (bf16[1,1,64,256]{3,2,1,0:T(8,128)(2,1)S(1)}, bf16[1,1,64,256]{3,2,1,0:T(8,128)(2,1)S(1)}, u32[]{:S(2)}, u32[]{:S(2)}) collective-permute-start(bf16[1,1,64,256]{3,2,1,0:T(8,128)(2,1)S(1)} %get-tuple-element.79), channel_id=1, source_target_pairs={{0,1},{2,3},{4,5},{6,7},{8,9},{10,11},{12,13},{14,15},{16,17},{18,... | collective-permute-start | bytes 98312 | tf_op jit(solution)/shard_map/ppermute | solution.py:17
  27.3 7.5 %collective-permute-start.4 = (bf16[1,8,64,256]{3,2,1,0:T(8,128)(2,1)S(1)}, bf16[1,8,64,256]{3,2,1,0:T(8,128)(2,1)S(1)}, u32[]{:S(2)}, u32[]{:S(2)}) collective-permute-start(bf16[1,8,64,256]{3,2,1,0:T(8,128)(2,1)S(1)} %add_convert_fusion.3), channel_id=1, source_target_pairs={{0,2},{2,4},{4,6},{6,8},{8,10},{10,12},{12,14},{14,16},{16,18},{18... | collective-permute-start | bytes 786440 | tf_op jit(solution)/shard_map/ppermute | solution.py:29
  34.8 3.3 %collective-permute-done.4 = bf16[1,8,64,256]{3,2,1,0:T(8,128)(2,1)S(1)} collective-permute-done((bf16[1,8,64,256]{3,2,1,0:T(8,128)(2,1)S(1)}, bf16[1,8,64,256]{3,2,1,0:T(8,128)(2,1)S(1)}, u32[]{:S(2)}, u32[]{:S(2)}) %collective-permute-start.4) | collective-permute-done | bytes 262176 | tf_op jit(solution)/shard_map/ppermute | solution.py:29
  38.2 1.3 collective-permute-start.6
  39.5 4.0 %collective-permute-start.5 = (bf16[1,1,64,256]{3,2,1,0:T(8,128)(2,1)S(1)}, bf16[1,1,64,256]{3,2,1,0:T(8,128)(2,1)S(1)}, u32[]{:S(2)}, u32[]{:S(2)}) collective-permute-start(bf16[1,1,64,256]{3,2,1,0:T(8,128)(2,1)S(1)} %get-tuple-element.75), channel_id=1, source_target_pairs={{0,1},{2,3},{4,5},{6,7},{8,9},{10,11},{12,13},{14,15},{16,17},{18,... | collective-permute-start | bytes 98312 | tf_op jit(solution)/shard_map/ppermute | solution.py:17
  47.1 1.3 collective-permute-start.8
  48.4 4.0 %collective-permute-start.7 = (bf16[1,1,64,256]{3,2,1,0:T(8,128)(2,1)S(1)}, bf16[1,1,64,256]{3,2,1,0:T(8,128)(2,1)S(1)}, u32[]{:S(2)}, u32[]{:S(2)}) collective-permute-start(bf16[1,1,64,256]{3,2,1,0:T(8,128)(2,1)S(1)} %get-tuple-element.71), channel_id=1, source_target_pairs={{0,1},{2,3},{4,5},{6,7},{8,9},{10,11},{12,13},{14,15},{16,17},{18,... | collective-permute-start | bytes 98312 | tf_op jit(solution)/shard_map/ppermute | solution.py:17
  56.1 8.2 %collective-permute-start.9 = (bf16[1,8,64,256]{3,2,1,0:T(8,128)(2,1)S(1)}, bf16[1,8,64,256]{3,2,1,0:T(8,128)(2,1)S(1)}, u32[]{:S(2)}, u32[]{:S(2)}) collective-permute-start(bf16[1,8,64,256]{3,2,1,0:T(8,128)(2,1)S(1)} %add_convert_fusion.1), channel_id=1, source_target_pairs={{0,2},{2,4},{4,6},{6,8},{8,10},{10,12},{12,14},{14,16},{16,18},{18... | collective-permute-start | bytes 786440 | tf_op jit(solution)/shard_map/ppermute | solution.py:29
  64.2 3.3 %collective-permute-done.9 = bf16[1,8,64,256]{3,2,1,0:T(8,128)(2,1)S(1)} collective-permute-done((bf16[1,8,64,256]{3,2,1,0:T(8,128)(2,1)S(1)}, bf16[1,8,64,256]{3,2,1,0:T(8,128)(2,1)S(1)}, u32[]{:S(2)}, u32[]{:S(2)}) %collective-permute-start.9) | collective-permute-done | bytes 262176 | tf_op jit(solution)/shard_map/ppermute | solution.py:29
  68.9 4.0 %collective-permute-start.11 = (bf16[1,1,64,256]{3,2,1,0:T(8,128)(2,1)S(1)}, bf16[1,1,64,256]{3,2,1,0:T(8,128)(2,1)S(1)}, u32[]{:S(2)}, u32[]{:S(2)}) collective-permute-start(bf16[1,1,64,256]{3,2,1,0:T(8,128)(2,1)S(1)} %get-tuple-element.67), channel_id=1, source_target_pairs={{0,1},{2,3},{4,5},{6,7},{8,9},{10,11},{12,13},{14,15},{16,17},{18,... | collective-permute-start | bytes 98312 | tf_op jit(solution)/shard_map/ppermute | solution.py:17
  79.3 4.6 %collective-permute-start.13 = (bf16[1,1,64,256]{3,2,1,0:T(8,128)(2,1)}, bf16[1,1,64,256]{3,2,1,0:T(8,128)(2,1)}, u32[]{:S(2)}, u32[]{:S(2)}) collective-permute-start(bf16[1,1,64,256]{3,2,1,0:T(8,128)(2,1)} %get-tuple-element.63), channel_id=1, source_target_pairs={{0,1},{2,3},{4,5},{6,7},{8,9},{10,11},{12,13},{14,15},{16,17},{18,... | collective-permute-start | bytes 98312 | tf_op jit(solution)/shard_map/ppermute | solution.py:17
  83.9 10.9 %collective-permute-start.10 = (bf16[1,8,64,256]{3,2,1,0:T(8,128)(2,1)}, bf16[1,8,64,256]{3,2,1,0:T(8,128)(2,1)S(1)}, u32[]{:S(2)}, u32[]{:S(2)}) collective-permute-start(bf16[1,8,64,256]{3,2,1,0:T(8,128)(2,1)} %bitcast.59), channel_id=1, source_target_pairs={{2,0},{4,2},{6,4},{8,6},{10,8},{12,10},{14,12},{16,14},{18,16},{20... | collective-permute-start | bytes 786440 | tf_op jit(solution)/shard_map/ppermute | solution.py:29
  101.0 4.2 %collective-permute-start.15 = (bf16[1,1,64,256]{3,2,1,0:T(8,128)(2,1)S(1)}, bf16[1,1,64,256]{3,2,1,0:T(8,128)(2,1)S(1)}, u32[]{:S(2)}, u32[]{:S(2)}) collective-permute-start(bf16[1,1,64,256]{3,2,1,0:T(8,128)(2,1)S(1)} %get-tuple-element.59), channel_id=1, source_target_pairs={{0,1},{2,3},{4,5},{6,7},{8,9},{10,11},{12,13},{14,15},{16,17},{18,... | collective-permute-start | bytes 98312 | tf_op jit(solution)/shard_map/ppermute | solution.py:17
  113.9 2.0 %fusion = bf16[2,9,256,256]{3,2,1,0:T(8,128)(2,1)} fusion(f32[1,9,256,256]{3,2,1,0:T(8,128)S(1)} %bitcast.520, f32[1,9,256,256]{3,2,1,0:T(8,128)S(1)} %bitcast.521), kind=kLoop, calls=%fused_computation.1 | loop fusion | flops 3538944 | bytes 7077888 | tf_op jit(solution)/shard_map/convert_element_type | solution.py:145
  115.9 7.6 %copy.8 = bf16[2,9,256,256]{2,1,0,3:T(8,128)(2,1)} copy(bf16[2,9,256,256]{3,2,1,0:T(8,128)(2,1)} %fusion) | data formatting | bytes 4718592
  123.4 5.6 %reshape.823 = bf16[256,4608]{1,0:T(8,128)(2,1)} reshape(bf16[256,2,9,256]{3,2,1,0:T(8,128)(2,1)} %bitcast.504) | data formatting | bytes 4718592
  129.1 1.3 collective-permute-start.18
  130.4 4.0 %collective-permute-start.17 = (bf16[1,1,64,256]{3,2,1,0:T(8,128)(2,1)S(1)}, bf16[1,1,64,256]{3,2,1,0:T(8,128)(2,1)S(1)}, u32[]{:S(2)}, u32[]{:S(2)}) collective-permute-start(bf16[1,1,64,256]{3,2,1,0:T(8,128)(2,1)S(1)} %get-tuple-element.55), channel_id=1, source_target_pairs={{0,1},{2,3},{4,5},{6,7},{8,9},{10,11},{12,13},{14,15},{16,17},{18,... | collective-permute-start | bytes 98312 | tf_op jit(solution)/shard_map/ppermute | solution.py:17
  139.1 28.6 %reduce-scatter.4.cloned.1.call-done = bf16[128,4608]{1,0:T(8,128)(2,1)} async-done(((bf16[256,4608]{1,0:T(8,128)(2,1)}), bf16[128,4608]{1,0:T(8,128)(2,1)}) %reduce-scatter.4.cloned.1.call-update) | async-done | bytes 1179664
  167.7 2.4 %reshape.824 = bf16[128,2,9,256]{3,2,1,0:T(8,128)(2,1)S(1)} reshape(bf16[128,4608]{1,0:T(8,128)(2,1)} %reduce-scatter.4.cloned.1.call-done) | data formatting | bytes 2359296
  170.2 1.7 copy.9
  171.8 1.6 convert_element_type.131
  (179 shorter events, 44.5 us)
Async XLA Ops:
  7.2 8.6 %copy-start = (bf16[2,9,256,256]{3,2,1,0:T(8,128)(2,1)S(1)}, bf16[2,9,256,256]{3,2,1,0:T(8,128)(2,1)}, u32[]{:S(2)}) copy-start(bf16[2,9,256,256]{3,2,1,0:T(8,128)(2,1)} %param.7) | copy-start | bytes 7077892
  7.2 160.6 %reduce-scatter.4.cloned.1.call-start = ((), (), s32[]{:S(2)}) async-start(), calls=%async_computation.1 | async-start | bytes 3538944
  8.2 5.3 %collective-permute-start.1 = (bf16[1,1,64,256]{3,2,1,0:T(8,128)(2,1)S(1)}, bf16[1,1,64,256]{3,2,1,0:T(8,128)(2,1)S(1)}, u32[]{:S(2)}, u32[]{:S(2)}) collective-permute-start(bf16[1,1,64,256]{3,2,1,0:T(8,128)(2,1)S(1)} %get-tuple-element.84), channel_id=1, source_target_pairs={{1,0},{3,2},{5,4},{7,6},{9,8},{11,10},{13,12},{15,14},{17,16},{19,... | collective-permute-start | bytes 98312 | tf_op jit(solution)/shard_map/ppermute | solution.py:19
  9.4 5.0 %collective-permute-start = (bf16[1,1,64,256]{3,2,1,0:T(8,128)(2,1)S(1)}, bf16[1,1,64,256]{3,2,1,0:T(8,128)(2,1)S(1)}, u32[]{:S(2)}, u32[]{:S(2)}) collective-permute-start(bf16[1,1,64,256]{3,2,1,0:T(8,128)(2,1)S(1)} %get-tuple-element.83), channel_id=1, source_target_pairs={{0,1},{2,3},{4,5},{6,7},{8,9},{10,11},{12,13},{14,15},{16,17},{18,... | collective-permute-start | bytes 98312 | tf_op jit(solution)/shard_map/ppermute | solution.py:17
  18.3 5.3 %collective-permute-start.3 = (bf16[1,1,64,256]{3,2,1,0:T(8,128)(2,1)S(1)}, bf16[1,1,64,256]{3,2,1,0:T(8,128)(2,1)S(1)}, u32[]{:S(2)}, u32[]{:S(2)}) collective-permute-start(bf16[1,1,64,256]{3,2,1,0:T(8,128)(2,1)S(1)} %get-tuple-element.80), channel_id=1, source_target_pairs={{1,0},{3,2},{5,4},{7,6},{9,8},{11,10},{13,12},{15,14},{17,16},{19,... | collective-permute-start | bytes 98312 | tf_op jit(solution)/shard_map/ppermute | solution.py:19
  19.6 5.0 %collective-permute-start.2 = (bf16[1,1,64,256]{3,2,1,0:T(8,128)(2,1)S(1)}, bf16[1,1,64,256]{3,2,1,0:T(8,128)(2,1)S(1)}, u32[]{:S(2)}, u32[]{:S(2)}) collective-permute-start(bf16[1,1,64,256]{3,2,1,0:T(8,128)(2,1)S(1)} %get-tuple-element.79), channel_id=1, source_target_pairs={{0,1},{2,3},{4,5},{6,7},{8,9},{10,11},{12,13},{14,15},{16,17},{18,... | collective-permute-start | bytes 98312 | tf_op jit(solution)/shard_map/ppermute | solution.py:17
  26.7 11.5 %copy-start.11 = (bf16[1,8,64,256]{3,2,1,0:T(8,128)(2,1)S(1)}, bf16[1,8,64,256]{3,2,1,0:T(8,128)(2,1)}, u32[]{:S(2)}) copy-start(bf16[1,8,64,256]{3,2,1,0:T(8,128)(2,1)} %param.8) | copy-start | bytes 786436
  27.3 10.8 %collective-permute-start.4 = (bf16[1,8,64,256]{3,2,1,0:T(8,128)(2,1)S(1)}, bf16[1,8,64,256]{3,2,1,0:T(8,128)(2,1)S(1)}, u32[]{:S(2)}, u32[]{:S(2)}) collective-permute-start(bf16[1,8,64,256]{3,2,1,0:T(8,128)(2,1)S(1)} %add_convert_fusion.3), channel_id=1, source_target_pairs={{0,2},{2,4},{4,6},{6,8},{8,10},{10,12},{12,14},{14,16},{16,18},{18... | collective-permute-start | bytes 786440 | tf_op jit(solution)/shard_map/ppermute | solution.py:29
  38.2 5.3 %collective-permute-start.6 = (bf16[1,1,64,256]{3,2,1,0:T(8,128)(2,1)S(1)}, bf16[1,1,64,256]{3,2,1,0:T(8,128)(2,1)S(1)}, u32[]{:S(2)}, u32[]{:S(2)}) collective-permute-start(bf16[1,1,64,256]{3,2,1,0:T(8,128)(2,1)S(1)} %get-tuple-element.76), channel_id=1, source_target_pairs={{1,0},{3,2},{5,4},{7,6},{9,8},{11,10},{13,12},{15,14},{17,16},{19,... | collective-permute-start | bytes 98312 | tf_op jit(solution)/shard_map/ppermute | solution.py:19
  39.5 5.0 %collective-permute-start.5 = (bf16[1,1,64,256]{3,2,1,0:T(8,128)(2,1)S(1)}, bf16[1,1,64,256]{3,2,1,0:T(8,128)(2,1)S(1)}, u32[]{:S(2)}, u32[]{:S(2)}) collective-permute-start(bf16[1,1,64,256]{3,2,1,0:T(8,128)(2,1)S(1)} %get-tuple-element.75), channel_id=1, source_target_pairs={{0,1},{2,3},{4,5},{6,7},{8,9},{10,11},{12,13},{14,15},{16,17},{18,... | collective-permute-start | bytes 98312 | tf_op jit(solution)/shard_map/ppermute | solution.py:17
  47.1 5.3 %collective-permute-start.8 = (bf16[1,1,64,256]{3,2,1,0:T(8,128)(2,1)S(1)}, bf16[1,1,64,256]{3,2,1,0:T(8,128)(2,1)S(1)}, u32[]{:S(2)}, u32[]{:S(2)}) collective-permute-start(bf16[1,1,64,256]{3,2,1,0:T(8,128)(2,1)S(1)} %get-tuple-element.72), channel_id=1, source_target_pairs={{1,0},{3,2},{5,4},{7,6},{9,8},{11,10},{13,12},{15,14},{17,16},{19,... | collective-permute-start | bytes 98312 | tf_op jit(solution)/shard_map/ppermute | solution.py:19
  48.4 5.0 %collective-permute-start.7 = (bf16[1,1,64,256]{3,2,1,0:T(8,128)(2,1)S(1)}, bf16[1,1,64,256]{3,2,1,0:T(8,128)(2,1)S(1)}, u32[]{:S(2)}, u32[]{:S(2)}) collective-permute-start(bf16[1,1,64,256]{3,2,1,0:T(8,128)(2,1)S(1)} %get-tuple-element.71), channel_id=1, source_target_pairs={{0,1},{2,3},{4,5},{6,7},{8,9},{10,11},{12,13},{14,15},{16,17},{18,... | collective-permute-start | bytes 98312 | tf_op jit(solution)/shard_map/ppermute | solution.py:17
  56.1 11.5 %collective-permute-start.9 = (bf16[1,8,64,256]{3,2,1,0:T(8,128)(2,1)S(1)}, bf16[1,8,64,256]{3,2,1,0:T(8,128)(2,1)S(1)}, u32[]{:S(2)}, u32[]{:S(2)}) collective-permute-start(bf16[1,8,64,256]{3,2,1,0:T(8,128)(2,1)S(1)} %add_convert_fusion.1), channel_id=1, source_target_pairs={{0,2},{2,4},{4,6},{6,8},{8,10},{10,12},{12,14},{14,16},{16,18},{18... | collective-permute-start | bytes 786440 | tf_op jit(solution)/shard_map/ppermute | solution.py:29
  67.6 44.9 %copy-start.1 = (bf16[1,8,64,256]{3,2,1,0:T(8,128)(2,1)}, bf16[1,8,64,256]{3,2,1,0:T(8,128)(2,1)S(1)}, u32[]{:S(2)}) copy-start(bf16[1,8,64,256]{3,2,1,0:T(8,128)(2,1)S(1)} %broadcast_select_fusion.1) | copy-start | bytes 786436
  67.6 5.3 %collective-permute-start.12 = (bf16[1,1,64,256]{3,2,1,0:T(8,128)(2,1)S(1)}, bf16[1,1,64,256]{3,2,1,0:T(8,128)(2,1)S(1)}, u32[]{:S(2)}, u32[]{:S(2)}) collective-permute-start(bf16[1,1,64,256]{3,2,1,0:T(8,128)(2,1)S(1)} %get-tuple-element.68), channel_id=1, source_target_pairs={{1,0},{3,2},{5,4},{7,6},{9,8},{11,10},{13,12},{15,14},{17,16},{19,... | collective-permute-start | bytes 98312 | tf_op jit(solution)/shard_map/ppermute | solution.py:19
  68.9 5.0 %collective-permute-start.11 = (bf16[1,1,64,256]{3,2,1,0:T(8,128)(2,1)S(1)}, bf16[1,1,64,256]{3,2,1,0:T(8,128)(2,1)S(1)}, u32[]{:S(2)}, u32[]{:S(2)}) collective-permute-start(bf16[1,1,64,256]{3,2,1,0:T(8,128)(2,1)S(1)} %get-tuple-element.67), channel_id=1, source_target_pairs={{0,1},{2,3},{4,5},{6,7},{8,9},{10,11},{12,13},{14,15},{16,17},{18,... | collective-permute-start | bytes 98312 | tf_op jit(solution)/shard_map/ppermute | solution.py:17
  78.0 16.8 %collective-permute-start.14 = (bf16[1,1,64,256]{3,2,1,0:T(8,128)(2,1)}, bf16[1,1,64,256]{3,2,1,0:T(8,128)(2,1)S(1)}, u32[]{:S(2)}, u32[]{:S(2)}) collective-permute-start(bf16[1,1,64,256]{3,2,1,0:T(8,128)(2,1)} %get-tuple-element.64), channel_id=1, source_target_pairs={{1,0},{3,2},{5,4},{7,6},{9,8},{11,10},{13,12},{15,14},{17,16},{19,... | collective-permute-start | bytes 98312 | tf_op jit(solution)/shard_map/ppermute | solution.py:19
  79.3 15.6 %collective-permute-start.13 = (bf16[1,1,64,256]{3,2,1,0:T(8,128)(2,1)}, bf16[1,1,64,256]{3,2,1,0:T(8,128)(2,1)}, u32[]{:S(2)}, u32[]{:S(2)}) collective-permute-start(bf16[1,1,64,256]{3,2,1,0:T(8,128)(2,1)} %get-tuple-element.63), channel_id=1, source_target_pairs={{0,1},{2,3},{4,5},{6,7},{8,9},{10,11},{12,13},{14,15},{16,17},{18,... | collective-permute-start | bytes 98312 | tf_op jit(solution)/shard_map/ppermute | solution.py:17
  83.9 15.0 %collective-permute-start.10 = (bf16[1,8,64,256]{3,2,1,0:T(8,128)(2,1)}, bf16[1,8,64,256]{3,2,1,0:T(8,128)(2,1)S(1)}, u32[]{:S(2)}, u32[]{:S(2)}) collective-permute-start(bf16[1,8,64,256]{3,2,1,0:T(8,128)(2,1)} %bitcast.59), channel_id=1, source_target_pairs={{2,0},{4,2},{6,4},{8,6},{10,8},{12,10},{14,12},{16,14},{18,16},{20... | collective-permute-start | bytes 786440 | tf_op jit(solution)/shard_map/ppermute | solution.py:29
  99.7 7.7 %collective-permute-start.16 = (bf16[1,1,64,256]{3,2,1,0:T(8,128)(2,1)S(1)}, bf16[1,1,64,256]{3,2,1,0:T(8,128)(2,1)S(1)}, u32[]{:S(2)}, u32[]{:S(2)}) collective-permute-start(bf16[1,1,64,256]{3,2,1,0:T(8,128)(2,1)S(1)} %get-tuple-element.60), channel_id=1, source_target_pairs={{1,0},{3,2},{5,4},{7,6},{9,8},{11,10},{13,12},{15,14},{17,16},{19,... | collective-permute-start | bytes 98312 | tf_op jit(solution)/shard_map/ppermute | solution.py:19
  101.0 6.4 %collective-permute-start.15 = (bf16[1,1,64,256]{3,2,1,0:T(8,128)(2,1)S(1)}, bf16[1,1,64,256]{3,2,1,0:T(8,128)(2,1)S(1)}, u32[]{:S(2)}, u32[]{:S(2)}) collective-permute-start(bf16[1,1,64,256]{3,2,1,0:T(8,128)(2,1)S(1)} %get-tuple-element.59), channel_id=1, source_target_pairs={{0,1},{2,3},{4,5},{6,7},{8,9},{10,11},{12,13},{14,15},{16,17},{18,... | collective-permute-start | bytes 98312 | tf_op jit(solution)/shard_map/ppermute | solution.py:17
  109.9 1.7 copy-start.10
  129.1 5.3 %collective-permute-start.18 = (bf16[1,1,64,256]{3,2,1,0:T(8,128)(2,1)S(1)}, bf16[1,1,64,256]{3,2,1,0:T(8,128)(2,1)S(1)}, u32[]{:S(2)}, u32[]{:S(2)}) collective-permute-start(bf16[1,1,64,256]{3,2,1,0:T(8,128)(2,1)S(1)} %get-tuple-element.56), channel_id=1, source_target_pairs={{1,0},{3,2},{5,4},{7,6},{9,8},{11,10},{13,12},{15,14},{17,16},{19,... | collective-permute-start | bytes 98312 | tf_op jit(solution)/shard_map/ppermute | solution.py:19
  130.4 5.0 %collective-permute-start.17 = (bf16[1,1,64,256]{3,2,1,0:T(8,128)(2,1)S(1)}, bf16[1,1,64,256]{3,2,1,0:T(8,128)(2,1)S(1)}, u32[]{:S(2)}, u32[]{:S(2)}) collective-permute-start(bf16[1,1,64,256]{3,2,1,0:T(8,128)(2,1)S(1)} %get-tuple-element.55), channel_id=1, source_target_pairs={{0,1},{2,3},{4,5},{6,7},{8,9},{10,11},{12,13},{14,15},{16,17},{18,... | collective-permute-start | bytes 98312 | tf_op jit(solution)/shard_map/ppermute | solution.py:17
  (8 other events, 8.0 us)
Sparse Core Ops, SparseCore 0:
  129.2 38.4 reduce-scatter.3
where the time goes:
time: 183 us; the launch traced here: 180 us
  starting transfers between devices  69.6 us (38%)
  waiting for transfers between devices  41.2 us (23%)
  local copies, waits for them, and re-layouts  22.1 us (12%)
  matrix products  21.9 us (12%)
  between operations  15.3 us (8%)
  other arithmetic  10.2 us (6%)
    ppermute x8, starting transfers between devices, with_halo(): lax.ppermute(tail, axis, [(i, (i + 1) % count) for i in range(ends)])  32.7 us
    unnamed x2, waiting for transfers between devices  28.6 us
    ppermute x3, starting transfers between devices, passed_along(): lax.ppermute(value, axis, [(source, source + steps) for source in range(i...  26.6 us
    unnamed x28, local copies, waits for them, and re-layouts  18.9 us
    dot_general x54, matrix products, convolve(): jnp.dot(window, kernel[tap_row * 3 + tap_col], preferred_element_type=jnp...  12.3 us
    ppermute x8, starting transfers between devices, with_halo(): lax.ppermute(head, axis, [((i + 1) % count, i) for i in range(ends)])  10.3 us
    ppermute x3, waiting for transfers between devices, passed_along(): lax.ppermute(value, axis, [(source, source + steps) for source in range(i...  6.58 us
    ppermute x8, waiting for transfers between devices, with_halo(): lax.ppermute(tail, axis, [(i, (i + 1) % count) for i in range(ends)])  5.97 us
  transfers between devices with their start and end apart: 20, of which 9 were waited for; matrix products, arithmetic and copies ran while one was open for 5% of the time, Pallas kernels for 0%

commit v1 on v0

v1 whole, which is shorter than its diff:
```python
import math

import jax
import jax.numpy as jnp
from jax import lax
from jax.experimental import pallas as pl
from jax.experimental.pallas import tpu as pltpu
from jax.sharding import PartitionSpec as P

MESH = pl.DeviceIdType.MESH
F32 = jnp.float32
BF16 = jnp.bfloat16
ROWS = 16
BAND = 8
W = 64
C = 256
PX = ROWS * W
BPX = BAND * W


def span(row, count):
    start = (row + 1) * W
    return pl.ds(start if isinstance(start, int) else pl.multiple_of(start, W), count * W)


def flat(row, count):
    start = row * W
    return pl.ds(start if isinstance(start, int) else pl.multiple_of(start, W), count * W)


def conv(src, weights, layer, row, count, back=False):
    n = count * W
    shifted = []
    for b in range(3):
        acc = None
        for a in range(3):
            window = src[span(row + a - 1, count), :]
            if back:
                term = lax.dot_general(
                    window,
                    weights[layer * 9 + (2 - a) * 3 + (2 - b)],
                    (((1,), (1,)), ((), ())),
                    preferred_element_type=F32,
                )
            else:
                term = jnp.dot(window, weights[layer * 9 + a * 3 + b], preferred_element_type=F32)
            acc = term if acc is None else acc + term
        shifted.append(acc)
    col = lax.broadcasted_iota(jnp.int32, (n, C), 0) % W
    left = jnp.where(col == 0, 0.0, pltpu.roll(shifted[0], 1, 0))
    right = jnp.where(col == W - 1, 0.0, pltpu.roll(shifted[2], n - 1, 0))
    return shifted[1] + left + right


def advance(src, dst, weights, layer, row, count, pre=None):
    value = conv(src, weights, layer, row, count)
    state = src[span(row, count), :].astype(F32)
    dst[span(row, count), :] = (state + 0.5 * value / (1.0 + jnp.exp(-value))).astype(BF16)
    if pre is not None:
        pre[flat(row, count), :] = value


def half_slope(value):
    s = 1.0 / (1.0 + jnp.exp(-value))
    return 0.5 * s * (1.0 + value * (1.0 - s))


def sweep_kernel(
    layers,
    guess, adj_guess, weights_hbm, net_input, cotangent,
    states_out, middle_out, delta1_out, delta2_out, adjoint_out,
    weights, x0, x1, x2, mid, mid3, end1, end2, adj, delta2, back, delta1, pre1, adj_own,
    load_sem, send_sem, halo_sem, x1_sem, x2_sem, adj_sem, out_sem,
):
    l = lax.axis_index("layer")
    r = lax.axis_index("rows")
    o = 1 - r
    even = l % 2 == 0
    first = l == 0
    last = l == layers - 1
    up = jnp.minimum(l + 1, layers - 1)
    down = jnp.maximum(l - 1, 0)
    own = r * BAND
    other = o * BAND

    loads = [
        pltpu.make_async_copy(guess, x0.at[span(own, BAND)], load_sem.at[0]),
        pltpu.make_async_copy(weights_hbm.at[pl.ds(0, 9)], weights.at[pl.ds(0, 9)], load_sem.at[1]),
        pltpu.make_async_copy(weights_hbm.at[pl.ds(9, 9)], weights.at[pl.ds(9, 9)], load_sem.at[2]),
    ]
    for copy in loads:
        copy.start()

    barrier = pltpu.get_barrier_semaphore()
    pl.semaphore_signal(barrier, inc=1, device_id=(l, o), device_id_type=MESH)

    @pl.when(jnp.logical_not(first))
    def _():
        pl.semaphore_signal(barrier, inc=1, device_id=(down, r), device_id_type=MESH)
        pl.semaphore_signal(barrier, inc=1, device_id=(down, o), device_id_type=MESH)

    @pl.when(jnp.logical_not(last))
    def _():
        pl.semaphore_signal(barrier, inc=1, device_id=(up, r), device_id_type=MESH)
        pl.semaphore_signal(barrier, inc=1, device_id=(up, o), device_id_type=MESH)

    zero = jnp.zeros((W, C), BF16)
    for buf in (x0, x1, x2, mid, mid3, delta2, delta1):
        buf[pl.ds(0, W), :] = zero
        buf[pl.ds((ROWS + 1) * W, W), :] = zero

    @pl.when(first | last)
    def _():
        pl.semaphore_wait(barrier, 3)

    @pl.when(jnp.logical_not(first | last))
    def _():
        pl.semaphore_wait(barrier, 5)

    def remote(src, dst, send, recv, device):
        return pltpu.make_async_remote_copy(
            src_ref=src, dst_ref=dst, send_sem=send_sem.at[send], recv_sem=recv,
            device_id=device, device_id_type=MESH,
        )

    edge = 6 + 2 * r
    inner1 = 9 * r
    inner2 = 10 * r
    other_edge = 6 + 2 * o

    loads[0].wait()
    halo = remote(x0.at[span(edge, 2)], x0.at[span(edge, 2)], 0, halo_sem.at[0], (l, o))
    halo.start()
    halo_in = remote(x0.at[span(other_edge, 2)], x0.at[span(other_edge, 2)], 0, halo_sem.at[0], (l, o))

    net1 = remote(net_input, x1.at[span(own, BAND)], 1, x1_sem.at[r], (l, o))
    net2 = remote(net_input, x2.at[span(own, BAND)], 2, x2_sem.at[r], (l, o))
    net1_here = pltpu.make_async_copy(net_input, x1.at[span(own, BAND)], x1_sem.at[r])
    net2_here = pltpu.make_async_copy(net_input, x2.at[span(own, BAND)], x2_sem.at[r])
    adj_last = remote(cotangent, adj.at[flat(own, BAND)], 3, adj_sem.at[r], (l, o))
    adj_last_here = pltpu.make_async_copy(cotangent, adj.at[flat(own, BAND)], adj_sem.at[r])
    adj_same = remote(adj_guess, adj.at[flat(own, BAND)], 4, adj_sem.at[r], (down, r))
    adj_cross = remote(adj_guess, adj.at[flat(own, BAND)], 5, adj_sem.at[r], (down, o))

    @pl.when(first)
    def _():
        net1_here.start()
        net1.start()
        net2_here.start()
        net2.start()

    loads[1].wait()
    advance(x0, mid, weights, 0, inner1, 7)
    loads[2].wait()
    advance(mid, end1, weights, 1, inner2, 6)

    def ship(buf, target, rows, count, send, sem, device):
        return remote(buf.at[span(rows, count)], target.at[span(rows, count)], send, sem, device)

    e1_inner_same = ship(end1, x1, inner2, 6, 6, x1_sem.at[r], (up, r))
    e1_inner_cross = ship(end1, x1, inner2, 6, 7, x1_sem.at[r], (up, o))
    e1_edge_same = ship(end1, x1, edge, 2, 8, x1_sem.at[r], (up, r))
    e1_edge_cross = ship(end1, x1, edge, 2, 9, x1_sem.at[r], (up, o))
    passes = jnp.logical_not(last)

    @pl.when(passes)
    def _():
        e1_inner_same.start()

        @pl.when(jnp.logical_not(even))
        def _():
            e1_inner_cross.start()

    halo_in.wait_recv()
    advance(x0, mid, weights, 0, 7, 2)
    advance(mid, end1, weights, 1, edge, 2)

    @pl.when(passes)
    def _():
        e1_edge_same.start()
        e1_edge_cross.start()

    @pl.when(last)
    def _():
        adj_last_here.start()
        adj_last.start()

    @pl.when(jnp.logical_not(first))
    def _():
        adj_same.start()
        adj_cross.start()

    x1_own = ship(end1, x1, own, BAND, 6, x1_sem.at[r], (l, o))
    x1_other = ship(end1, x1, other, BAND, 6, x1_sem.at[o], (l, o))
    x1_edge = ship(end1, x1, other_edge, 2, 6, x1_sem.at[o], (l, o))
    e2_inner_same = ship(end2, x2, inner2, 6, 10, x2_sem.at[r], (up, r))
    e2_inner_cross = ship(end2, x2, inner2, 6, 11, x2_sem.at[r], (up, o))
    e2_edge_same = ship(end2, x2, edge, 2, 12, x2_sem.at[r], (up, r))
    e2_edge_cross = ship(end2, x2, edge, 2, 13, x2_sem.at[r], (up, o))
    e2_low = ship(end2, x2, 0, BAND, 10, x2_sem.at[0], (up, r))
    e2_high = ship(end2, x2, BAND, BAND, 11, x2_sem.at[1], (up, r))

    @pl.when(jnp.logical_not(even))
    def _():
        x1_own.wait_recv()
        advance(x1, mid, weights, 0, inner1, 7)
        advance(mid, end2, weights, 1, inner2, 6)

        @pl.when(passes)
        def _():
            e2_inner_same.start()
            e2_inner_cross.start()

        x1_edge.wait_recv()
        advance(x1, mid, weights, 0, 7, 2)
        advance(mid, end2, weights, 1, edge, 2)

        @pl.when(passes)
        def _():
            e2_edge_same.start()
            e2_edge_cross.start()

    @pl.when(even)
    def _():
        x1_own.wait_recv()
        x1_other.wait_recv()
        advance(x1, mid, weights, 0, 0, ROWS)
        advance(mid, end2, weights, 1, 0, BAND)
        e2_low.start()
        advance(mid, end2, weights, 1, BAND, BAND)
        e2_high.start()

    x2_own = ship(end1, x2, own, BAND, 6, x2_sem.at[r], (l, o))
    x2_other = ship(end1, x2, other, BAND, 6, x2_sem.at[o], (l, o))
    x2_own.wait_recv()
    x2_other.wait_recv()
    outs = [pltpu.make_async_copy(x2.at[span(0, ROWS)], states_out, out_sem.at[0])]
    outs[-1].start()
    advance(x2, mid3, weights, 0, 0, ROWS, pre1)
    outs.append(pltpu.make_async_copy(mid3.at[span(0, ROWS)], middle_out, out_sem.at[1]))
    outs[-1].start()

    value = conv(mid3, weights, 1, 0, ROWS)
    remote(cotangent, adj.at[flat(own, BAND)], 3, adj_sem.at[r], (l, o)).wait_recv()
    remote(cotangent, adj.at[flat(other, BAND)], 3, adj_sem.at[o], (l, o)).wait_recv()
    delta2[span(0, ROWS), :] = (half_slope(value) * adj[...].astype(F32)).astype(BF16)
    half = pl.ds(pl.multiple_of(r * 128, 128), 128)
    outs.append(pltpu.make_async_copy(delta2.at[span(0, ROWS), half], delta2_out, out_sem.at[2]))
    outs[-1].start()

    value = conv(delta2, weights, 1, 0, ROWS, back=True)
    value = (adj[...].astype(F32) + value).astype(BF16)
    back[...] = value
    delta1[span(0, ROWS), :] = (half_slope(pre1[...]) * value.astype(F32)).astype(BF16)
    outs.append(pltpu.make_async_copy(delta1.at[span(0, ROWS), half], delta1_out, out_sem.at[3]))
    outs[-1].start()

    value = conv(delta1, weights, 0, own, BAND, back=True)
    adj_own[...] = (back[flat(own, BAND), :].astype(F32) + value).astype(BF16)
    outs.append(pltpu.make_async_copy(adj_own, adjoint_out, out_sem.at[4]))
    outs[-1].start()

    halo.wait_send()

    @pl.when(first)
    def _():
        net1.wait_send()
        net2.wait_send()

    @pl.when(last)
    def _():
        adj_last.wait_send()

    @pl.when(jnp.logical_not(first))
    def _():
        adj_same.wait_send()
        adj_cross.wait_send()

    @pl.when(passes)
    def _():
        e1_inner_same.wait_send()
        e1_edge_same.wait_send()
        e1_edge_cross.wait_send()

        @pl.when(jnp.logical_not(even))
        def _():
            e1_inner_cross.wait_send()
            e2_inner_same.wait_send()
            e2_inner_cross.wait_send()
            e2_edge_same.wait_send()
            e2_edge_cross.wait_send()

    @pl.when(even)
    def _():
        e2_low.wait_send()
        e2_high.wait_send()

    for copy in outs:
        copy.wait()


def grad_kernel(
    scale,
    states, middle, delta1, delta2, adjoint,
    states_out, adjoint_out, grad_out,
    x, m, d1, d2, wide, grads, sem, out_sem,
):
    r = lax.axis_index("rows")
    loads = [
        pltpu.make_async_copy(middle, m, sem.at[0]),
        pltpu.make_async_copy(delta2, d2, sem.at[1]),
        pltpu.make_async_copy(states, x, sem.at[2]),
        pltpu.make_async_copy(delta1, d1, sem.at[3]),
    ]
    for copy in loads:
        copy.start()
    outs = [
        pltpu.make_async_copy(states.at[flat(r * BAND, BAND)], states_out, out_sem.at[0]),
        pltpu.make_async_copy(adjoint, adjoint_out, out_sem.at[1]),
    ]
    for copy in outs:
        copy.start()
    zero = jnp.zeros((W, 384), BF16)
    for layer in range(2):
        wide[layer, pl.ds(0, W), :] = zero
        wide[layer, pl.ds((ROWS + 1) * W, W), :] = zero
    col = lax.broadcasted_iota(jnp.int32, (PX, 128), 0) % W
    for layer, image, delta, pair in ((1, m, d2, 0), (0, x, d1, 2)):
        loads[pair].wait()
        loads[pair + 1].wait()
        value = delta[...].astype(F32)
        after = jnp.where(col == W - 1, 0.0, pltpu.roll(value, PX - 1, 0))
        before = jnp.where(col == 0, 0.0, pltpu.roll(value, 1, 0))
        wide[layer, pl.ds(W, PX), 0:128] = after.astype(BF16)
        wide[layer, pl.ds(W, PX), 128:256] = delta[...]
        wide[layer, pl.ds(W, PX), 256:384] = before.astype(BF16)
        side = jnp.concatenate([wide[layer, pl.ds((2 - a) * W, PX), :] for a in range(3)], axis=1)
        terms = lax.dot_general(
            image[...], side, (((0,), (0,)), ((), ())), preferred_element_type=F32
        )
        for tap in range(9):
            grads[layer, tap] = terms[:, tap * 128 : (tap + 1) * 128] * scale
        outs.append(pltpu.make_async_copy(grads.at[layer], grad_out.at[layer], out_sem.at[2 + layer]))
        outs[-1].start()
    for copy in outs:
        copy.wait()


def solution(mesh):
    layers = mesh.shape["layer"]
    scale = 1.0 / math.sqrt(PX)
    hbm = pl.BlockSpec(memory_space=pl.ANY)
    image = lambda rows: pltpu.VMEM((rows * W, C), BF16)

    def local(guess, adj_guess, weights, net_input, cotangent):
        args = (
            guess.reshape(BPX, C),
            adj_guess.reshape(BPX, C),
            weights.reshape(18, C, C),
            net_input.reshape(BPX, C),
            cotangent.reshape(BPX, C),
        )
        sds = jax.ShapeDtypeStruct
        states, middle, delta1, delta2, adjoint = pl.pallas_call(
            lambda *refs: sweep_kernel(layers, *refs),
            out_shape=(
                sds((PX, C), BF16), sds((PX, C), BF16), sds((PX, 128), BF16), sds((PX, 128), BF16),
                sds((BPX, C), BF16),
            ),
            in_specs=[hbm] * 5,
            out_specs=[hbm] * 5,
            scratch_shapes=[
                pltpu.VMEM((18, C, C), BF16),
                image(18), image(18), image(18), image(18), image(18), image(18), image(18),
                image(16), image(18), image(16), image(18),
                pltpu.VMEM((PX, C), F32),
                image(8),
                pltpu.SemaphoreType.DMA((3,)),
                pltpu.SemaphoreType.DMA((14,)),
                pltpu.SemaphoreType.DMA((1,)),
                pltpu.SemaphoreType.DMA((2,)),
                pltpu.SemaphoreType.DMA((2,)),
                pltpu.SemaphoreType.DMA((2,)),
                pltpu.SemaphoreType.DMA((5,)),
            ],
            compiler_params=pltpu.CompilerParams(
                collective_id=0, has_side_effects=True, vmem_limit_bytes=48 << 20
            ),
            name="sweeps",
        )(*args)
        states, adjoint, grads = pl.pallas_call(
            lambda *refs: grad_kernel(scale, *refs),
            out_shape=(sds((BPX, C), BF16), sds((BPX, C), BF16), sds((2, 9, C, 128), F32)),
            in_specs=[hbm] * 5,
            out_specs=[hbm] * 3,
            scratch_shapes=[
                image(16), image(16),
                pltpu.VMEM((PX, 128), BF16), pltpu.VMEM((PX, 128), BF16),
                pltpu.VMEM((2, 18 * W, 384), BF16),
                pltpu.VMEM((2, 9, C, 128), F32),
                pltpu.SemaphoreType.DMA((4,)),
                pltpu.SemaphoreType.DMA((4,)),
            ],
            compiler_params=pltpu.CompilerParams(vmem_limit_bytes=48 << 20),
            name="weight_grads",
        )(states, middle, delta1, delta2, adjoint)
        shape = (1, 1, BAND, W, C)
        return states.reshape(shape), adjoint.reshape(shape), grads

    in_specs = (
        P("layer", None, "rows", None, None),
        P("layer", None, "rows", None, None),
        P("layer", None, None, None),
        P(None, "rows", None, None),
        P(None, "rows", None, None),
    )
    out_specs = (
        P("layer", None, "rows", None, None),
        P("layer", None, "rows", None, None),
        P("layer", None, None, "rows"),
    )
    return jax.shard_map(local, mesh=mesh, in_specs=in_specs, out_specs=out_specs, check_vma=False)
```

time: 183 us -> 46.6 us (0.25); the launches traced: 180 us -> 46.3 us
  starting transfers between devices: 69.6 us -> 0 us
  waiting for transfers between devices: 41.2 us -> 0 us
  Pallas kernels: 0 us -> 40 us
  matrix products: 21.9 us -> 0 us
  local copies, waits for them, and re-layouts: 22.1 us -> 5.46 us
  between operations: 15.3 us -> 0.81 us
  other arithmetic: 10.2 us -> 0 us
    ppermute x19 -> x0, starting transfers between devices: 69.6 us -> none  [the longest x8 32.7 us: with_halo(): lax.ppermute(tail, axis, [(i, (i + 1) % count) for i in range(ends)])]
    pallas_call x0 -> x2, Pallas kernels: none -> 40 us  [the longest x1 37 us: local(): pl.pallas_call(lambda *refs: sweep_kernel(layers, *refs), out_shape=(sds(...]
    unnamed x2 -> x0, waiting for transfers between devices: 28.6 us -> none
    dot_general x90 -> x0, matrix products: 21.9 us -> none  [the longest x54 12.3 us: convolve(): jnp.dot(window, kernel[tap_row * 3 + tap_col], preferred_element_type=jnp...]
    unnamed x28 -> x10, local copies, waits for them, and re-layouts: 18.9 us -> 5.46 us
    ppermute x19 -> x0, waiting for transfers between devices: 12.6 us -> none  [the longest x3 6.58 us: passed_along(): lax.ppermute(value, axis, [(source, source + steps) for source in range(i...]
    convert_element_type x9 -> x0, other arithmetic: 5.71 us -> none  [the longest x1 1.97 us: local(): partial_value.astype(jnp.bfloat16)]
    concatenate x16 -> x0, other arithmetic: 3.64 us -> none  [with_halo(): jnp.concatenate([lax.ppermute(tail, axis, [(i, (i + 1) % count) for i in...]
  transfers between devices with their start and end apart: 20 -> 0, of which waited for: 9 -> 0; matrix products, arithmetic and copies ran while one was open for 5% -> 0% of each run, Pallas kernels for 0% -> 0%
where the time goes in v1:
time: 46.6 us; the launch traced here: 46.3 us
  Pallas kernels  40 us (86%)
  local copies, waits for them, and re-layouts  5.46 us (12%)
  between operations  0.81 us (2%)
    pallas_call x1, Pallas kernels, local(): pl.pallas_call(lambda *refs: sweep_kernel(layers, *refs), out_shape=(sds(...  37 us
    unnamed x10, local copies, waits for them, and re-layouts  5.46 us
    pallas_call x1, Pallas kernels, local(): pl.pallas_call(lambda *refs: grad_kernel(scale, *refs), out_shape=(sds((B...  3.02 us

profile of v1, /device:TPU:97, one launch (start us, length us, event | category | flops | bytes accessed | tf_op | source)
XLA Modules:
  0.0 46.3 jit_solution(1554366772149505329)
XLA Ops:
  0.6 0.0 copy-start
  0.6 1.7 %copy-done = bf16[2,9,256,256]{3,2,1,0:T(8,128)(2,1)S(1)} copy-done((bf16[2,9,256,256]{3,2,1,0:T(8,128)(2,1)S(1)}, bf16[2,9,256,256]{3,2,1,0:T(8,128)(2,1)}, u32[]{:S(2)}) %copy-start) | copy-done | bytes 2359320
  2.3 0.0 copy-start.1
  2.3 0.9 %copy-done.1 = bf16[1,1,8,64,256]{4,3,2,1,0:T(8,128)(2,1)S(1)} copy-done((bf16[1,1,8,64,256]{4,3,2,1,0:T(8,128)(2,1)S(1)}, bf16[1,1,8,64,256]{4,3,2,1,0:T(8,128)(2,1)}, u32[]{:S(2)}) %copy-start.1) | copy-done | bytes 262168
  3.2 0.0 copy-start.2
  3.3 0.9 %copy-done.2 = bf16[1,1,8,64,256]{4,3,2,1,0:T(8,128)(2,1)S(1)} copy-done((bf16[1,1,8,64,256]{4,3,2,1,0:T(8,128)(2,1)S(1)}, bf16[1,1,8,64,256]{4,3,2,1,0:T(8,128)(2,1)}, u32[]{:S(2)}) %copy-start.2) | copy-done | bytes 262168
  4.2 0.0 copy-start.3
  4.2 0.9 %copy-done.3 = bf16[1,8,64,256]{3,2,1,0:T(8,128)(2,1)S(1)} copy-done((bf16[1,8,64,256]{3,2,1,0:T(8,128)(2,1)S(1)}, bf16[1,8,64,256]{3,2,1,0:T(8,128)(2,1)}, u32[]{:S(2)}) %copy-start.3) | copy-done | bytes 262168
  5.1 0.0 copy-start.4
  5.2 0.9 %copy-done.4 = bf16[1,8,64,256]{3,2,1,0:T(8,128)(2,1)S(1)} copy-done((bf16[1,8,64,256]{3,2,1,0:T(8,128)(2,1)S(1)}, bf16[1,8,64,256]{3,2,1,0:T(8,128)(2,1)}, u32[]{:S(2)}) %copy-start.4) | copy-done | bytes 262168
  6.1 37.0 %sweeps.1 = (bf16[1024,256]{1,0:T(8,128)(2,1)S(1)}, bf16[1024,256]{1,0:T(8,128)(2,1)S(1)}, bf16[1024,128]{1,0:T(8,128)(2,1)S(1)}, bf16[1024,128]{1,0:T(8,128)(2,1)S(1)}, bf16[512,256]{1,0:T(8,128)(2,1)S(1)}) custom-call(bf16[512,256]{1,0:T(8,128)(2,1)S(1)} %bitcast.8, bf16[512,256]{1,0:T(8,128)(2,1)S(1)} %bitcast.9, bf16[18,256,256]{2,1,0:T(8,128)(2,1)S(1)} %bitcast.7, ...), custom_call_target="tpu_custom_call" | custom-call | tf_op jit(solution)/shard_map/sweeps/pallas_call | solution.py:364
  43.1 3.0 %weight_grads.1 = (bf16[512,256]{1,0:T(8,128)(2,1)}, bf16[512,256]{1,0:T(8,128)(2,1)}, f32[2,9,256,128]{3,2,1,0:T(8,128)}) custom-call(bf16[1024,256]{1,0:T(8,128)(2,1)S(1)} %get-tuple-element.11.refs_0_, bf16[1024,256]{1,0:T(8,128)(2,1)S(1)} %get-tuple-element.12.refs_1_, bf16[1024,128]{1,0:T(8,128)(2,1)S(1)} %get-tuple-element.13.refs_2_, ...), custom_call_target="tpu_custom_call" | custom-call | tf_op jit(solution)/shard_map/weight_grads/pallas_call | solution.py:391
Async XLA Ops:
  0.6 1.7 %copy-start = (bf16[2,9,256,256]{3,2,1,0:T(8,128)(2,1)S(1)}, bf16[2,9,256,256]{3,2,1,0:T(8,128)(2,1)}, u32[]{:S(2)}) copy-start(bf16[2,9,256,256]{3,2,1,0:T(8,128)(2,1)} %param.7) | copy-start | bytes 7077892
  2.3 0.9 %copy-start.1 = (bf16[1,1,8,64,256]{4,3,2,1,0:T(8,128)(2,1)S(1)}, bf16[1,1,8,64,256]{4,3,2,1,0:T(8,128)(2,1)}, u32[]{:S(2)}) copy-start(bf16[1,1,8,64,256]{4,3,2,1,0:T(8,128)(2,1)} %param.5) | copy-start | bytes 786436
  3.2 0.9 %copy-start.2 = (bf16[1,1,8,64,256]{4,3,2,1,0:T(8,128)(2,1)S(1)}, bf16[1,1,8,64,256]{4,3,2,1,0:T(8,128)(2,1)}, u32[]{:S(2)}) copy-start(bf16[1,1,8,64,256]{4,3,2,1,0:T(8,128)(2,1)} %param.6) | copy-start | bytes 786436
  4.2 0.9 %copy-start.3 = (bf16[1,8,64,256]{3,2,1,0:T(8,128)(2,1)S(1)}, bf16[1,8,64,256]{3,2,1,0:T(8,128)(2,1)}, u32[]{:S(2)}) copy-start(bf16[1,8,64,256]{3,2,1,0:T(8,128)(2,1)} %param.8) | copy-start | bytes 786436
  5.1 0.9 %copy-start.4 = (bf16[1,8,64,256]{3,2,1,0:T(8,128)(2,1)S(1)}, bf16[1,8,64,256]{3,2,1,0:T(8,128)(2,1)}, u32[]{:S(2)}) copy-start(bf16[1,8,64,256]{3,2,1,0:T(8,128)(2,1)} %param.9) | copy-start | bytes 786436

commit v2 on v1

--- a/solution.py
+++ b/solution.py
@@ -69,17 +69,22 @@
     layers,
     guess, adj_guess, weights_hbm, net_input, cotangent,
     states_out, middle_out, delta1_out, delta2_out, adjoint_out,
-    weights, x0, x1, x2, mid, mid3, end1, end2, adj, delta2, back, delta1, pre1, adj_own,
+    weights, x0, x1, x2, mid, mid3, end1, end2, adj, delta2, back, delta1, pre1, pre2, adj_own,
     load_sem, send_sem, halo_sem, x1_sem, x2_sem, adj_sem, out_sem,
 ):
     l = lax.axis_index("layer")
     r = lax.axis_index("rows")
     o = 1 - r
     even = l % 2 == 0
+    odd = l % 2 == 1
     first = l == 0
     last = l == layers - 1
+    passes = jnp.logical_not(last)
+    takes = jnp.logical_not(first)
     up = jnp.minimum(l + 1, layers - 1)
     down = jnp.maximum(l - 1, 0)
+    t = (r + l) % 2
+    s = (r + l + 1) % 2
     own = r * BAND
     other = o * BAND
 
@@ -123,127 +128,133 @@
             device_id=device, device_id_type=MESH,
         )
 
-    edge = 6 + 2 * r
-    inner1 = 9 * r
-    inner2 = 10 * r
-    other_edge = 6 + 2 * o
-
-    loads[0].wait()
-    halo = remote(x0.at[span(edge, 2)], x0.at[span(edge, 2)], 0, halo_sem.at[0], (l, o))
-    halo.start()
-    halo_in = remote(x0.at[span(other_edge, 2)], x0.at[span(other_edge, 2)], 0, halo_sem.at[0], (l, o))
-
-    net1 = remote(net_input, x1.at[span(own, BAND)], 1, x1_sem.at[r], (l, o))
-    net2 = remote(net_input, x2.at[span(own, BAND)], 2, x2_sem.at[r], (l, o))
-    net1_here = pltpu.make_async_copy(net_input, x1.at[span(own, BAND)], x1_sem.at[r])
-    net2_here = pltpu.make_async_copy(net_input, x2.at[span(own, BAND)], x2_sem.at[r])
-    adj_last = remote(cotangent, adj.at[flat(own, BAND)], 3, adj_sem.at[r], (l, o))
-    adj_last_here = pltpu.make_async_copy(cotangent, adj.at[flat(own, BAND)], adj_sem.at[r])
-    adj_same = remote(adj_guess, adj.at[flat(own, BAND)], 4, adj_sem.at[r], (down, r))
-    adj_cross = remote(adj_guess, adj.at[flat(own, BAND)], 5, adj_sem.at[r], (down, o))
-
-    @pl.when(first)
-    def _():
-        net1_here.start()
-        net1.start()
-        net2_here.start()
-        net2.start()
-
-    loads[1].wait()
-    advance(x0, mid, weights, 0, inner1, 7)
-    loads[2].wait()
-    advance(mid, end1, weights, 1, inner2, 6)
+    edge = lambda band: 6 + 2 * band
+    inner = lambda band: 10 * band
 
     def ship(buf, target, rows, count, send, sem, device):
         return remote(buf.at[span(rows, count)], target.at[span(rows, count)], send, sem, device)
 
-    e1_inner_same = ship(end1, x1, inner2, 6, 6, x1_sem.at[r], (up, r))
-    e1_inner_cross = ship(end1, x1, inner2, 6, 7, x1_sem.at[r], (up, o))
-    e1_edge_same = ship(end1, x1, edge, 2, 8, x1_sem.at[r], (up, r))
-    e1_edge_cross = ship(end1, x1, edge, 2, 9, x1_sem.at[r], (up, o))
-    passes = jnp.logical_not(last)
-
-    @pl.when(passes)
-    def _():
-        e1_inner_same.start()
-
-        @pl.when(jnp.logical_not(even))
-        def _():
-            e1_inner_cross.start()
-
-    halo_in.wait_recv()
-    advance(x0, mid, weights, 0, 7, 2)
-    advance(mid, end1, weights, 1, edge, 2)
-
-    @pl.when(passes)
-    def _():
-        e1_edge_same.start()
-        e1_edge_cross.start()
+    loads[0].wait()
+    halo = ship(x0, x0, edge(r), 2, 0, halo_sem.at[0], (l, o))
+    halo.start()
+    halo_in = ship(x0, x0, edge(o), 2, 0, halo_sem.at[0], (l, o))
+
+    inner_here = pl.ds(pl.multiple_of(2 * r * W, W), 6 * W)
+    edge_here = pl.ds(pl.multiple_of((6 - 6 * r) * W, W), 2 * W)
+    nets = [
+        remote(net_input, x1.at[span(own, BAND)], 1, x1_sem.at[0], (l, o)),
+        remote(net_input.at[inner_here], x2.at[span(inner(r), 6)], 2, x2_sem.at[r, 0], (l, o)),
+        remote(net_input.at[edge_here], x2.at[span(edge(r), 2)], 3, x2_sem.at[r, 1], (l, o)),
+    ]
+    nets_here = [
+        pltpu.make_async_copy(net_input.at[edge_here], x1.at[span(edge(r), 2)], x1_sem.at[1]),
+        pltpu.make_async_copy(net_input.at[inner_here], x2.at[span(inner(r), 6)], x2_sem.at[r, 0]),
+        pltpu.make_async_copy(net_input.at[edge_here], x2.at[span(edge(r), 2)], x2_sem.at[r, 1]),
+    ]
+    adj_last = remote(cotangent, adj.at[flat(own, BAND)], 4, adj_sem.at[r], (l, o))
+    adj_last_here = pltpu.make_async_copy(cotangent, adj.at[flat(own, BAND)], adj_sem.at[r])
+    adj_cross = remote(adj_guess, adj.at[flat(own, BAND)], 5, adj_sem.at[r], (down, o))
+    adj_same = remote(adj_guess, adj.at[flat(own, BAND)], 6, adj_sem.at[r], (down, r))
+
+    @pl.when(first)
+    def _():
+        for copy in nets + nets_here:
+            copy.start()
 
     @pl.when(last)
     def _():
+        adj_last.start()
         adj_last_here.start()
-        adj_last.start()
-
-    @pl.when(jnp.logical_not(first))
-    def _():
-        adj_same.start()
-        adj_cross.start()
-
-    x1_own = ship(end1, x1, own, BAND, 6, x1_sem.at[r], (l, o))
-    x1_other = ship(end1, x1, other, BAND, 6, x1_sem.at[o], (l, o))
-    x1_edge = ship(end1, x1, other_edge, 2, 6, x1_sem.at[o], (l, o))
-    e2_inner_same = ship(end2, x2, inner2, 6, 10, x2_sem.at[r], (up, r))
-    e2_inner_cross = ship(end2, x2, inner2, 6, 11, x2_sem.at[r], (up, o))
-    e2_edge_same = ship(end2, x2, edge, 2, 12, x2_sem.at[r], (up, r))
-    e2_edge_cross = ship(end2, x2, edge, 2, 13, x2_sem.at[r], (up, o))
-    e2_low = ship(end2, x2, 0, BAND, 10, x2_sem.at[0], (up, r))
-    e2_high = ship(end2, x2, BAND, BAND, 11, x2_sem.at[1], (up, r))
-
-    @pl.when(jnp.logical_not(even))
-    def _():
-        x1_own.wait_recv()
-        advance(x1, mid, weights, 0, inner1, 7)
-        advance(mid, end2, weights, 1, inner2, 6)
-
+
+    def sweep(src, dst, band, rest, edge_in, send):
+        advance(src, mid, weights, 0, 9 * band, 7)
+        rest()
+        advance(mid, dst, weights, 1, inner(band), 6)
+        send(inner(band), 6, 0)
+        edge_in.wait_recv()
+        advance(src, mid, weights, 0, 7, 2)
+        advance(mid, dst, weights, 1, edge(band), 2)
+        send(edge(band), 2, 1)
+
+    def send1(rows, count, part):
         @pl.when(passes)
         def _():
-            e2_inner_same.start()
-            e2_inner_cross.start()
-
-        x1_edge.wait_recv()
-        advance(x1, mid, weights, 0, 7, 2)
-        advance(mid, end2, weights, 1, edge, 2)
-
+            ship(end1, x1, rows, count, 8 + part, x1_sem.at[0], (up, t)).start()
+            if part:
+                ship(end1, x1, rows, count, 10, x1_sem.at[1], (up, 1 - t)).start()
+
+        if not part:
+
+            @pl.when(even)
+            def _():
+                ship(end1, x1, rows, count, 17, x1_sem.at[2], (up, 1 - t)).start()
+
+    loads[1].wait()
+    sweep(x0, end1, r, loads[2].wait, halo_in, send1)
+
+    @pl.when(takes)
+    def _():
+        adj_cross.start()
+
+    @pl.when(odd)
+    def _():
+        adj_same.start()
+
+    def send2(rows, count, part):
         @pl.when(passes)
         def _():
-            e2_edge_same.start()
-            e2_edge_cross.start()
-
-    @pl.when(even)
-    def _():
-        x1_own.wait_recv()
-        x1_other.wait_recv()
-        advance(x1, mid, weights, 0, 0, ROWS)
-        advance(mid, end2, weights, 1, 0, BAND)
-        e2_low.start()
-        advance(mid, end2, weights, 1, BAND, BAND)
-        e2_high.start()
-
-    x2_own = ship(end1, x2, own, BAND, 6, x2_sem.at[r], (l, o))
-    x2_other = ship(end1, x2, other, BAND, 6, x2_sem.at[o], (l, o))
-    x2_own.wait_recv()
-    x2_other.wait_recv()
+            ship(end2, x2, rows, count, 11 + part, x2_sem.at[s, part], (up, o)).start()
+
+        @pl.when(even)
+        def _():
+            ship(end2, x2, rows, count, 13 + part, x2_sem.at[s, part], (up, r)).start()
+
+    ship(end1, x1, s * BAND, BAND, 8, x1_sem.at[0], (l, o)).wait_recv()
+    x1_edge = ship(end1, x1, edge(1 - s), 2, 10, x1_sem.at[1], (l, o))
+    sweep(x1, end2, s, lambda: None, x1_edge, send2)
+
+    adj_in = remote(adj_guess, adj.at[flat(other, BAND)], 5, adj_sem.at[o], (l, o))
+    adj_on = remote(adj.at[flat(other, BAND)], adj.at[flat(other, BAND)], 7, adj_sem.at[o], (l, o))
+
+    @pl.when(odd & passes)
+    def _():
+        ship(end1, x1, inner(1 - s), 6, 17, x1_sem.at[2], (l, o)).wait_recv()
+        advance(x1, mid, weights, 0, 9 * (1 - s), 7)
+        advance(mid, end2, weights, 1, (1 - s) * BAND, BAND)
+        for part, rows, count in ((0, inner(1 - s), 6), (1, edge(1 - s), 2)):
+            ship(end2, x2, rows, count, 15 + part, x2_sem.at[1 - s, part], (up, o)).start()
+        adj_in.wait_recv()
+        adj_on.start()
+
+    @pl.when(odd & last)
+    def _():
+        ship(end1, x1, inner(1 - s), 6, 17, x1_sem.at[2], (l, o)).wait_recv()
+
+    for part, rows, count in ((0, inner(o), 6), (1, edge(o), 2)):
+        ship(end2, x2, rows, count, 11, x2_sem.at[o, part], (l, o)).wait_recv()
+    advance(x2, mid3, weights, 0, 9 * o, 7, pre1)
+
+    def second(row, count):
+        value = conv(mid3, weights, 1, row, count)
+        pre2[flat(row, count), :] = value
+
+    second(inner(o), 6)
+    for part, rows, count in ((0, inner(r), 6), (1, edge(r), 2)):
+        ship(end2, x2, rows, count, 11, x2_sem.at[r, part], (l, o)).wait_recv()
     outs = [pltpu.make_async_copy(x2.at[span(0, ROWS)], states_out, out_sem.at[0])]
     outs[-1].start()
-    advance(x2, mid3, weights, 0, 0, ROWS, pre1)
+    advance(x2, mid3, weights, 0, 7 * r, 9, pre1)
     outs.append(pltpu.make_async_copy(mid3.at[span(0, ROWS)], middle_out, out_sem.at[1]))
     outs[-1].start()
-
-    value = conv(mid3, weights, 1, 0, ROWS)
-    remote(cotangent, adj.at[flat(own, BAND)], 3, adj_sem.at[r], (l, o)).wait_recv()
-    remote(cotangent, adj.at[flat(other, BAND)], 3, adj_sem.at[o], (l, o)).wait_recv()
-    delta2[span(0, ROWS), :] = (half_slope(value) * adj[...].astype(F32)).astype(BF16)
+    second(6 * r, 10)
+
+    remote(cotangent, adj.at[flat(own, BAND)], 4, adj_sem.at[r], (l, o)).wait_recv()
+
+    @pl.when(even | last)
+    def _():
+        adj_in.wait_recv()
+
+    delta2[span(0, ROWS), :] = (half_slope(pre2[...]) * adj[...].astype(F32)).astype(BF16)
     half = pl.ds(pl.multiple_of(r * 128, 128), 128)
     outs.append(pltpu.make_async_copy(delta2.at[span(0, ROWS), half], delta2_out, out_sem.at[2]))
     outs[-1].start()
@@ -264,36 +275,42 @@
 
     @pl.when(first)
     def _():
-        net1.wait_send()
-        net2.wait_send()
+        for copy in nets:
+            copy.wait_send()
 
     @pl.when(last)
     def _():
         adj_last.wait_send()
 
-    @pl.when(jnp.logical_not(first))
+    @pl.when(takes)
+    def _():
+        adj_cross.wait_send()
+
+    @pl.when(odd)
     def _():
         adj_same.wait_send()
-        adj_cross.wait_send()
+
+    @pl.when(odd & passes)
+    def _():
+        adj_on.wait_send()
 
     @pl.when(passes)
     def _():
-        e1_inner_same.wait_send()
-        e1_edge_same.wait_send()
-        e1_edge_cross.wait_send()
-
-        @pl.when(jnp.logical_not(even))
-        def _():
-            e1_inner_cross.wait_send()
-            e2_inner_same.wait_send()
-            e2_inner_cross.wait_send()
-            e2_edge_same.wait_send()
-            e2_edge_cross.wait_send()
+        for rows, count, send in ((inner(r), 6, 8), (edge(r), 2, 9), (edge(r), 2, 10)):
+            ship(end1, x1, rows, count, send, x1_sem.at[0], (l, o)).wait_send()
+        for rows, count, send in ((inner(s), 6, 11), (edge(s), 2, 12)):
+            ship(end2, x2, rows, count, send, x2_sem.at[0, 0], (l, o)).wait_send()
 
     @pl.when(even)
     def _():
-        e2_low.wait_send()
-        e2_high.wait_send()
+        ship(end1, x1, inner(r), 6, 17, x1_sem.at[2], (l, o)).wait_send()
+        for rows, count, send in ((inner(s), 6, 13), (edge(s), 2, 14)):
+            ship(end2, x2, rows, count, send, x2_sem.at[0, 0], (l, o)).wait_send()
+
+    @pl.when(odd & passes)
+    def _():
+        for rows, count, send in ((inner(1 - s), 6, 15), (edge(1 - s), 2, 16)):
+            ship(end2, x2, rows, count, send, x2_sem.at[0, 0], (l, o)).wait_send()
 
     for copy in outs:
         copy.wait()
@@ -303,7 +320,7 @@
     scale,
     states, middle, delta1, delta2, adjoint,
     states_out, adjoint_out, grad_out,
-    x, m, d1, d2, wide, grads, sem, out_sem,
+    x, m, d1, d2, adj, wide, grads, sem, out_sem,
 ):
     r = lax.axis_index("rows")
     loads = [
@@ -311,15 +328,11 @@
         pltpu.make_async_copy(delta2, d2, sem.at[1]),
         pltpu.make_async_copy(states, x, sem.at[2]),
         pltpu.make_async_copy(delta1, d1, sem.at[3]),
+        pltpu.make_async_copy(adjoint, adj, sem.at[4]),
     ]
     for copy in loads:
         copy.start()
-    outs = [
-        pltpu.make_async_copy(states.at[flat(r * BAND, BAND)], states_out, out_sem.at[0]),
-        pltpu.make_async_copy(adjoint, adjoint_out, out_sem.at[1]),
-    ]
-    for copy in outs:
-        copy.start()
+    outs = []
     zero = jnp.zeros((W, 384), BF16)
     for layer in range(2):
         wide[layer, pl.ds(0, W), :] = zero
@@ -328,6 +341,12 @@
     for layer, image, delta, pair in ((1, m, d2, 0), (0, x, d1, 2)):
         loads[pair].wait()
         loads[pair + 1].wait()
+        if layer == 0:
+            loads[4].wait()
+            outs.append(pltpu.make_async_copy(x.at[flat(r * BAND, BAND)], states_out, out_sem.at[0]))
+            outs.append(pltpu.make_async_copy(adj, adjoint_out, out_sem.at[1]))
+            for copy in outs[-2:]:
+                copy.start()
         value = delta[...].astype(F32)
         after = jnp.where(col == W - 1, 0.0, pltpu.roll(value, PX - 1, 0))
         before = jnp.where(col == 0, 0.0, pltpu.roll(value, 1, 0))
@@ -374,17 +393,18 @@
                 image(18), image(18), image(18), image(18), image(18), image(18), image(18),
                 image(16), image(18), image(16), image(18),
                 pltpu.VMEM((PX, C), F32),
+                pltpu.VMEM((PX, C), F32),
                 image(8),
                 pltpu.SemaphoreType.DMA((3,)),
-                pltpu.SemaphoreType.DMA((14,)),
+                pltpu.SemaphoreType.DMA((18,)),
                 pltpu.SemaphoreType.DMA((1,)),
-                pltpu.SemaphoreType.DMA((2,)),
-                pltpu.SemaphoreType.DMA((2,)),
+                pltpu.SemaphoreType.DMA((3,)),
+                pltpu.SemaphoreType.DMA((2, 2)),
                 pltpu.SemaphoreType.DMA((2,)),
                 pltpu.SemaphoreType.DMA((5,)),
             ],
             compiler_params=pltpu.CompilerParams(
-                collective_id=0, has_side_effects=True, vmem_limit_bytes=48 << 20
+                collective_id=0, has_side_effects=True, vmem_limit_bytes=60 << 20
             ),
             name="sweeps",
         )(*args)
@@ -396,12 +416,13 @@
             scratch_shapes=[
                 image(16), image(16),
                 pltpu.VMEM((PX, 128), BF16), pltpu.VMEM((PX, 128), BF16),
+                image(8),
                 pltpu.VMEM((2, 18 * W, 384), BF16),
                 pltpu.VMEM((2, 9, C, 128), F32),
-                pltpu.SemaphoreType.DMA((4,)),
+                pltpu.SemaphoreType.DMA((5,)),
                 pltpu.SemaphoreType.DMA((4,)),
             ],
-            compiler_params=pltpu.CompilerParams(vmem_limit_bytes=48 << 20),
+            compiler_params=pltpu.CompilerParams(vmem_limit_bytes=56 << 20),
             name="weight_grads",
         )(states, middle, delta1, delta2, adjoint)
         shape = (1, 1, BAND, W, C)

time: 46.6 us -> 35.2 us (0.76)
  the two profiles are of different devices: /device:TPU:97 before, /device:TPU:6 now
where the time goes in v2:
time: 35.2 us; the launch traced here: 35.1 us
  Pallas kernels  34.5 us (98%)
  between operations  0.64 us (2%)
    pallas_call x1, Pallas kernels, local(): pl.pallas_call(lambda *refs: sweep_kernel(layers, *refs), out_shape=(sds(...  30.5 us
    pallas_call x1, Pallas kernels, local(): pl.pallas_call(lambda *refs: grad_kernel(scale, *refs), out_shape=(sds((B...  4 us

profile of v2, /device:TPU:6, one launch (start us, length us, event | category | flops | bytes accessed | tf_op | source)
XLA Modules:
  0.0 35.1 jit_solution(5024193461873121980)
XLA Ops:
  0.6 30.5 %sweeps.1 = (bf16[1024,256]{1,0:T(8,128)(2,1)}, bf16[1024,256]{1,0:T(8,128)(2,1)}, bf16[1024,128]{1,0:T(8,128)(2,1)}, bf16[1024,128]{1,0:T(8,128)(2,1)}, bf16[512,256]{1,0:T(8,128)(2,1)}) custom-call(bf16[512,256]{1,0:T(8,128)(2,1)} %bitcast.8, bf16[512,256]{1,0:T(8,128)(2,1)} %bitcast.9, bf16[18,256,256]{2,1,0:T(8,128)(2,1)} %bitcast.7, ...), custom_call_target="tpu_custom_call" | custom-call | tf_op jit(solution)/shard_map/sweeps/pallas_call | solution.py:383
  31.1 4.0 %weight_grads.1 = (bf16[512,256]{1,0:T(8,128)(2,1)}, bf16[512,256]{1,0:T(8,128)(2,1)}, f32[2,9,256,128]{3,2,1,0:T(8,128)}) custom-call(bf16[1024,256]{1,0:T(8,128)(2,1)} %get-tuple-element.11.refs_0_, bf16[1024,256]{1,0:T(8,128)(2,1)} %get-tuple-element.12.refs_1_, bf16[1024,128]{1,0:T(8,128)(2,1)} %get-tuple-element.13.refs_2_, ...), custom_call_target="tpu_custom_call" | custom-call | tf_op jit(solution)/shard_map/weight_grads/pallas_call | solution.py:411

commit v3 on v2

--- a/solution.py
+++ b/solution.py
@@ -84,7 +84,7 @@
     up = jnp.minimum(l + 1, layers - 1)
     down = jnp.maximum(l - 1, 0)
     t = (r + l) % 2
-    s = (r + l + 1) % 2
+    s = jnp.where(first, r, (r + l + 1) % 2)
     own = r * BAND
     other = o * BAND
 
@@ -129,7 +129,10 @@
         )
 
     edge = lambda band: 6 + 2 * band
+    near = lambda band: 4 + 6 * band
+    far = lambda band: 12 * band
     inner = lambda band: 10 * band
+    parts = ((far, 4), (near, 2), (edge, 2))
 
     def ship(buf, target, rows, count, send, sem, device):
         return remote(buf.at[span(rows, count)], target.at[span(rows, count)], send, sem, device)
@@ -139,130 +142,193 @@
     halo.start()
     halo_in = ship(x0, x0, edge(o), 2, 0, halo_sem.at[0], (l, o))
 
-    inner_here = pl.ds(pl.multiple_of(2 * r * W, W), 6 * W)
-    edge_here = pl.ds(pl.multiple_of((6 - 6 * r) * W, W), 2 * W)
-    nets = [
-        remote(net_input, x1.at[span(own, BAND)], 1, x1_sem.at[0], (l, o)),
-        remote(net_input.at[inner_here], x2.at[span(inner(r), 6)], 2, x2_sem.at[r, 0], (l, o)),
-        remote(net_input.at[edge_here], x2.at[span(edge(r), 2)], 3, x2_sem.at[r, 1], (l, o)),
-    ]
-    nets_here = [
-        pltpu.make_async_copy(net_input.at[edge_here], x1.at[span(edge(r), 2)], x1_sem.at[1]),
-        pltpu.make_async_copy(net_input.at[inner_here], x2.at[span(inner(r), 6)], x2_sem.at[r, 0]),
-        pltpu.make_async_copy(net_input.at[edge_here], x2.at[span(edge(r), 2)], x2_sem.at[r, 1]),
-    ]
-    adj_last = remote(cotangent, adj.at[flat(own, BAND)], 4, adj_sem.at[r], (l, o))
+    net_at = lambda rows, count: net_input.at[flat(rows - own, count)]
+    net1 = remote(net_at(edge(r), 2), x1.at[span(edge(r), 2)], 1, x1_sem.at[1], (l, o))
+    nets2 = [
+        remote(net_at(rows(r), count), x2.at[span(rows(r), count)], 2 + part, x2_sem.at[r, part], (l, o))
+        for part, (rows, count) in enumerate(parts)
+    ]
+    nets_here = [pltpu.make_async_copy(net_input, x1.at[span(own, BAND)], x1_sem.at[0])] + [
+        pltpu.make_async_copy(net_at(rows(r), count), x2.at[span(rows(r), count)], x2_sem.at[r, part])
+        for part, (rows, count) in enumerate(parts)
+    ]
+    adj_last = remote(cotangent, adj.at[flat(own, BAND)], 5, adj_sem.at[r], (l, o))
     adj_last_here = pltpu.make_async_copy(cotangent, adj.at[flat(own, BAND)], adj_sem.at[r])
-    adj_cross = remote(adj_guess, adj.at[flat(own, BAND)], 5, adj_sem.at[r], (down, o))
-    adj_same = remote(adj_guess, adj.at[flat(own, BAND)], 6, adj_sem.at[r], (down, r))
+    adj_cross = remote(adj_guess, adj.at[flat(own, BAND)], 6, adj_sem.at[r], (down, o))
+    adj_same = remote(adj_guess, adj.at[flat(own, BAND)], 7, adj_sem.at[r], (down, r))
 
     @pl.when(first)
     def _():
-        for copy in nets + nets_here:
+        net1.start()
+        for copy in nets_here:
             copy.start()
 
-    @pl.when(last)
-    def _():
-        adj_last.start()
-        adj_last_here.start()
+    @pl.when(takes)
+    def _():
+        adj_cross.start()
+
+    @pl.when(odd)
+    def _():
+        adj_same.start()
 
     def sweep(src, dst, band, rest, edge_in, send):
         advance(src, mid, weights, 0, 9 * band, 7)
         rest()
         advance(mid, dst, weights, 1, inner(band), 6)
-        send(inner(band), 6, 0)
+        send(False)
         edge_in.wait_recv()
         advance(src, mid, weights, 0, 7, 2)
         advance(mid, dst, weights, 1, edge(band), 2)
-        send(edge(band), 2, 1)
-
-    def send1(rows, count, part):
+        send(True)
+
+    e1_inner = ship(end1, x1, inner(r), 6, 9, x1_sem.at[0], (up, t))
+    e1_edge = ship(end1, x1, edge(r), 2, 10, x1_sem.at[0], (up, t))
+    e1_cross = ship(end1, x1, edge(r), 2, 11, x1_sem.at[1], (up, 1 - t))
+    e1_rest = ship(end1, x1, inner(r), 6, 12, x1_sem.at[2], (up, o))
+
+    def send1(late):
         @pl.when(passes)
         def _():
-            ship(end1, x1, rows, count, 8 + part, x1_sem.at[0], (up, t)).start()
-            if part:
-                ship(end1, x1, rows, count, 10, x1_sem.at[1], (up, 1 - t)).start()
-
-        if not part:
+            if late:
+                e1_cross.start()
+                e1_edge.start()
+            else:
+                e1_inner.start()
+
+        if late:
 
             @pl.when(even)
             def _():
-                ship(end1, x1, rows, count, 17, x1_sem.at[2], (up, 1 - t)).start()
+                e1_rest.start()
 
     loads[1].wait()
     sweep(x0, end1, r, loads[2].wait, halo_in, send1)
 
-    @pl.when(takes)
-    def _():
-        adj_cross.start()
-
-    @pl.when(odd)
-    def _():
-        adj_same.start()
-
-    def send2(rows, count, part):
+    @pl.when(first)
+    def _():
+        for copy in nets2[::-1]:
+            copy.start()
+
+    @pl.when(last)
+    def _():
+        adj_last.start()
+        adj_last_here.start()
+
+    adj_in = remote(adj_guess, adj.at[flat(other, BAND)], 6, adj_sem.at[o], (l, o))
+    adj_on = remote(adj.at[flat(other, BAND)], adj.at[flat(other, BAND)], 8, adj_sem.at[o], (l, o))
+
+    e2 = [
+        ship(end2, x2, rows(s), count, 13 + part, x2_sem.at[s, part], (up, o))
+        for part, (rows, count) in enumerate(parts)
+    ]
+    e2_same = [
+        ship(end2, x2, rows(s), count, 16 + part, x2_sem.at[s, part], (up, r))
+        for part, (rows, count) in enumerate(parts)
+    ]
+
+    def send2(late):
+        which = slice(2, 3) if late else slice(0, 2)
+
         @pl.when(passes)
         def _():
-            ship(end2, x2, rows, count, 11 + part, x2_sem.at[s, part], (up, o)).start()
-
-        @pl.when(even)
+            for copy in e2[which]:
+                copy.start()
+
+    q = 1 - s
+    x1_own = ship(end1, x1, s * BAND, BAND, 9, x1_sem.at[0], (l, o))
+    x1_edge = ship(end1, x1, edge(q), 2, 11, x1_sem.at[1], (l, o))
+    x1_rest = ship(end1, x1, inner(q), 6, 12, x1_sem.at[2], (l, o))
+    e2_other = [
+        ship(end2, x2, rows(q), count, 19 + part, x2_sem.at[q, part], (up, o))
+        for part, (rows, count) in enumerate(parts)
+    ]
+
+    distant = l % 16 == 15
+
+    def pass_adjoint(here):
+        @pl.when(here & passes)
         def _():
-            ship(end2, x2, rows, count, 13 + part, x2_sem.at[s, part], (up, r)).start()
-
-    ship(end1, x1, s * BAND, BAND, 8, x1_sem.at[0], (l, o)).wait_recv()
-    x1_edge = ship(end1, x1, edge(1 - s), 2, 10, x1_sem.at[1], (l, o))
-    sweep(x1, end2, s, lambda: None, x1_edge, send2)
-
-    adj_in = remote(adj_guess, adj.at[flat(other, BAND)], 5, adj_sem.at[o], (l, o))
-    adj_on = remote(adj.at[flat(other, BAND)], adj.at[flat(other, BAND)], 7, adj_sem.at[o], (l, o))
-
-    @pl.when(odd & passes)
-    def _():
-        ship(end1, x1, inner(1 - s), 6, 17, x1_sem.at[2], (l, o)).wait_recv()
-        advance(x1, mid, weights, 0, 9 * (1 - s), 7)
-        advance(mid, end2, weights, 1, (1 - s) * BAND, BAND)
-        for part, rows, count in ((0, inner(1 - s), 6), (1, edge(1 - s), 2)):
-            ship(end2, x2, rows, count, 15 + part, x2_sem.at[1 - s, part], (up, o)).start()
+            adj_in.wait_recv()
+            adj_on.start()
+
+    @pl.when(even)
+    def _():
+        x1_own.wait_recv()
+        x1_edge.wait_recv()
+        advance(x1, mid, weights, 0, 7 * s, 9)
+        advance(mid, end2, weights, 1, s * BAND, BAND)
+        for part in (2, 1, 0):
+            e2_same[part].start()
+            e2[part].start()
+
+    @pl.when(odd)
+    def _():
+        x1_own.wait_recv()
+        sweep(x1, end2, s, lambda: None, x1_edge, send2)
+        pass_adjoint(jnp.logical_not(distant))
+        x1_rest.wait_recv()
+
+        @pl.when(passes)
+        def _():
+            advance(x1, mid, weights, 0, 3 + 6 * q, 4)
+            advance(mid, end2, weights, 1, 4 + 4 * q, 4)
+            for copy in e2_other[1:]:
+                copy.start()
+            advance(x1, mid, weights, 0, 13 * q, 3)
+            advance(mid, end2, weights, 1, far(q), 4)
+            e2_other[0].start()
+
+        pass_adjoint(distant)
+
+    x2_in = lambda band, part: ship(
+        end2, x2, parts[part][0](band), parts[part][1], 13, x2_sem.at[band, part], (l, o)
+    ).wait_recv()
+    f = jnp.where(l < 2, r, o)
+    g = 1 - f
+    for part in range(3):
+        x2_in(f, part)
+    advance(x2, mid3, weights, 0, 9 * f, 7, pre1)
+
+    def second(row, count):
+        pre2[flat(row, count), :] = conv(mid3, weights, 1, row, count)
+
+    def turn(row, count):
+        value = half_slope(pre2[flat(row, count), :]) * adj[flat(row, count), :].astype(F32)
+        delta2[span(row, count), :] = value.astype(BF16)
+
+    def turn_back(row, count):
+        value = conv(delta2, weights, 1, row, count, back=True)
+        value = (adj[flat(row, count), :].astype(F32) + value).astype(BF16)
+        back[flat(row, count), :] = value
+        value = half_slope(pre1[flat(row, count), :]) * value.astype(F32)
+        delta1[span(row, count), :] = value.astype(BF16)
+
+    second(inner(f), 6)
+    x2_in(g, 1)
+    x2_in(g, 2)
+    advance(x2, mid3, weights, 0, 7 - 2 * f, 4, pre1)
+    second(6, 4)
+    remote(cotangent, adj.at[flat(own, BAND)], 5, adj_sem.at[r], (l, o)).wait_recv()
+
+    @pl.when(even | last)
+    def _():
         adj_in.wait_recv()
-        adj_on.start()
-
-    @pl.when(odd & last)
-    def _():
-        ship(end1, x1, inner(1 - s), 6, 17, x1_sem.at[2], (l, o)).wait_recv()
-
-    for part, rows, count in ((0, inner(o), 6), (1, edge(o), 2)):
-        ship(end2, x2, rows, count, 11, x2_sem.at[o, part], (l, o)).wait_recv()
-    advance(x2, mid3, weights, 0, 9 * o, 7, pre1)
-
-    def second(row, count):
-        value = conv(mid3, weights, 1, row, count)
-        pre2[flat(row, count), :] = value
-
-    second(inner(o), 6)
-    for part, rows, count in ((0, inner(r), 6), (1, edge(r), 2)):
-        ship(end2, x2, rows, count, 11, x2_sem.at[r, part], (l, o)).wait_recv()
+
+    turn(6 * f, 10)
+    turn_back(7 * f, 9)
+
+    x2_in(g, 0)
+    half = pl.ds(pl.multiple_of(r * 128, 128), 128)
     outs = [pltpu.make_async_copy(x2.at[span(0, ROWS)], states_out, out_sem.at[0])]
     outs[-1].start()
-    advance(x2, mid3, weights, 0, 7 * r, 9, pre1)
+    advance(x2, mid3, weights, 0, 11 * g, 5, pre1)
     outs.append(pltpu.make_async_copy(mid3.at[span(0, ROWS)], middle_out, out_sem.at[1]))
     outs[-1].start()
-    second(6 * r, 10)
-
-    remote(cotangent, adj.at[flat(own, BAND)], 4, adj_sem.at[r], (l, o)).wait_recv()
-
-    @pl.when(even | last)
-    def _():
-        adj_in.wait_recv()
-
-    delta2[span(0, ROWS), :] = (half_slope(pre2[...]) * adj[...].astype(F32)).astype(BF16)
-    half = pl.ds(pl.multiple_of(r * 128, 128), 128)
+    second(10 * g, 6)
+    turn(10 * g, 6)
     outs.append(pltpu.make_async_copy(delta2.at[span(0, ROWS), half], delta2_out, out_sem.at[2]))
     outs[-1].start()
-
-    value = conv(delta2, weights, 1, 0, ROWS, back=True)
-    value = (adj[...].astype(F32) + value).astype(BF16)
-    back[...] = value
-    delta1[span(0, ROWS), :] = (half_slope(pre1[...]) * value.astype(F32)).astype(BF16)
+    turn_back(9 * g, 7)
     outs.append(pltpu.make_async_copy(delta1.at[span(0, ROWS), half], delta1_out, out_sem.at[3]))
     outs[-1].start()
 
@@ -272,45 +338,20 @@
     outs[-1].start()
 
     halo.wait_send()
-
-    @pl.when(first)
-    def _():
-        for copy in nets:
-            copy.wait_send()
-
-    @pl.when(last)
-    def _():
-        adj_last.wait_send()
-
-    @pl.when(takes)
-    def _():
-        adj_cross.wait_send()
-
-    @pl.when(odd)
-    def _():
-        adj_same.wait_send()
-
-    @pl.when(odd & passes)
-    def _():
-        adj_on.wait_send()
-
-    @pl.when(passes)
-    def _():
-        for rows, count, send in ((inner(r), 6, 8), (edge(r), 2, 9), (edge(r), 2, 10)):
-            ship(end1, x1, rows, count, send, x1_sem.at[0], (l, o)).wait_send()
-        for rows, count, send in ((inner(s), 6, 11), (edge(s), 2, 12)):
-            ship(end2, x2, rows, count, send, x2_sem.at[0, 0], (l, o)).wait_send()
-
-    @pl.when(even)
-    def _():
-        ship(end1, x1, inner(r), 6, 17, x1_sem.at[2], (l, o)).wait_send()
-        for rows, count, send in ((inner(s), 6, 13), (edge(s), 2, 14)):
-            ship(end2, x2, rows, count, send, x2_sem.at[0, 0], (l, o)).wait_send()
-
-    @pl.when(odd & passes)
-    def _():
-        for rows, count, send in ((inner(1 - s), 6, 15), (edge(1 - s), 2, 16)):
-            ship(end2, x2, rows, count, send, x2_sem.at[0, 0], (l, o)).wait_send()
+    for here, copies in (
+        (first, [net1] + nets2),
+        (last, [adj_last]),
+        (takes, [adj_cross]),
+        (odd, [adj_same]),
+        (odd & passes, [adj_on] + e2_other),
+        (passes, [e1_inner, e1_edge, e1_cross] + e2),
+        (even, [e1_rest] + e2_same),
+    ):
+
+        @pl.when(here)
+        def _(copies=copies):
+            for copy in copies:
+                copy.wait_send()
 
     for copy in outs:
         copy.wait()
@@ -396,10 +437,10 @@
                 pltpu.VMEM((PX, C), F32),
                 image(8),
                 pltpu.SemaphoreType.DMA((3,)),
-                pltpu.SemaphoreType.DMA((18,)),
+                pltpu.SemaphoreType.DMA((22,)),
                 pltpu.SemaphoreType.DMA((1,)),
                 pltpu.SemaphoreType.DMA((3,)),
-                pltpu.SemaphoreType.DMA((2, 2)),
+                pltpu.SemaphoreType.DMA((2, 3)),
                 pltpu.SemaphoreType.DMA((2,)),
                 pltpu.SemaphoreType.DMA((5,)),
             ],

time: 35.2 us -> 32.1 us (0.912)
  the two profiles are of different devices: /device:TPU:6 before, /device:TPU:97 now
where the time goes in v3:
time: 32.1 us; the launch traced here: 31.7 us
  Pallas kernels  30.9 us (96%)
  between operations  0.8 us (2%)
    pallas_call x1, Pallas kernels, local(): pl.pallas_call(lambda *refs: sweep_kernel(layers, *refs), out_shape=(sds(...  26.9 us
    pallas_call x1, Pallas kernels, local(): pl.pallas_call(lambda *refs: grad_kernel(scale, *refs), out_shape=(sds((B...  4 us

profile of v3, /device:TPU:97, one launch (start us, length us, event | category | flops | bytes accessed | tf_op | source)
XLA Modules:
  0.0 31.7 jit_solution(12890418147695800154)
XLA Ops:
  0.6 26.9 %sweeps.1 = (bf16[1024,256]{1,0:T(8,128)(2,1)}, bf16[1024,256]{1,0:T(8,128)(2,1)}, bf16[1024,128]{1,0:T(8,128)(2,1)}, bf16[1024,128]{1,0:T(8,128)(2,1)}, bf16[512,256]{1,0:T(8,128)(2,1)}) custom-call(bf16[512,256]{1,0:T(8,128)(2,1)} %bitcast.8, bf16[512,256]{1,0:T(8,128)(2,1)} %bitcast.9, bf16[18,256,256]{2,1,0:T(8,128)(2,1)} %bitcast.7, ...), custom_call_target="tpu_custom_call" | custom-call | tf_op jit(solution)/shard_map/sweeps/pallas_call | solution.py:424
  27.6 4.0 %weight_grads.1 = (bf16[512,256]{1,0:T(8,128)(2,1)}, bf16[512,256]{1,0:T(8,128)(2,1)}, f32[2,9,256,128]{3,2,1,0:T(8,128)}) custom-call(bf16[1024,256]{1,0:T(8,128)(2,1)} %get-tuple-element.11.refs_0_, bf16[1024,256]{1,0:T(8,128)(2,1)} %get-tuple-element.12.refs_1_, bf16[1024,128]{1,0:T(8,128)(2,1)} %get-tuple-element.13.refs_2_, ...), custom_call_target="tpu_custom_call" | custom-call | tf_op jit(solution)/shard_map/weight_grads/pallas_call | solution.py:452

commit v4 on v3

--- a/solution.py
+++ b/solution.py
@@ -52,24 +52,28 @@
     return shifted[1] + left + right
 
 
-def advance(src, dst, weights, layer, row, count, pre=None):
+def sigmoid(value):
+    return 1.0 / (1.0 + jnp.exp(-value))
+
+
+def half_slope(value, s):
+    return 0.5 * s * (1.0 + value * (1.0 - s))
+
+
+def advance(src, dst, weights, layer, row, count, slope=None):
     value = conv(src, weights, layer, row, count)
+    s = sigmoid(value)
     state = src[span(row, count), :].astype(F32)
-    dst[span(row, count), :] = (state + 0.5 * value / (1.0 + jnp.exp(-value))).astype(BF16)
-    if pre is not None:
-        pre[flat(row, count), :] = value
-
-
-def half_slope(value):
-    s = 1.0 / (1.0 + jnp.exp(-value))
-    return 0.5 * s * (1.0 + value * (1.0 - s))
+    dst[span(row, count), :] = (state + 0.5 * value * s).astype(BF16)
+    if slope is not None:
+        slope[flat(row, count), :] = half_slope(value, s)
 
 
 def sweep_kernel(
     layers,
     guess, adj_guess, weights_hbm, net_input, cotangent,
     states_out, middle_out, delta1_out, delta2_out, adjoint_out,
-    weights, x0, x1, x2, mid, mid3, end1, end2, adj, delta2, back, delta1, pre1, pre2, adj_own,
+    weights, x0, x1, x2, mid, mid3, end1, end2, adj, delta2, back, delta1, slope1, slope2,
     load_sem, send_sem, halo_sem, x1_sem, x2_sem, adj_sem, out_sem,
 ):
     l = lax.axis_index("layer")
@@ -204,11 +208,6 @@
     loads[1].wait()
     sweep(x0, end1, r, loads[2].wait, halo_in, send1)
 
-    @pl.when(first)
-    def _():
-        for copy in nets2[::-1]:
-            copy.start()
-
     @pl.when(last)
     def _():
         adj_last.start()
@@ -260,6 +259,11 @@
         for part in (2, 1, 0):
             e2_same[part].start()
             e2[part].start()
+
+        @pl.when(first)
+        def _():
+            for copy in nets2[::-1]:
+                copy.start()
 
     @pl.when(odd)
     def _():
@@ -287,55 +291,51 @@
     g = 1 - f
     for part in range(3):
         x2_in(f, part)
-    advance(x2, mid3, weights, 0, 9 * f, 7, pre1)
+    advance(x2, mid3, weights, 0, 9 * f, 7, slope1)
 
     def second(row, count):
-        pre2[flat(row, count), :] = conv(mid3, weights, 1, row, count)
-
-    def turn(row, count):
-        value = half_slope(pre2[flat(row, count), :]) * adj[flat(row, count), :].astype(F32)
-        delta2[span(row, count), :] = value.astype(BF16)
+        value = conv(mid3, weights, 1, row, count)
+        return half_slope(value, sigmoid(value))
+
+    def turn(row, count, slope):
+        value = (slope * adj[flat(row, count), :].astype(F32)).astype(BF16)
+        delta2[span(row, count), :] = value
+        delta2_out[flat(row, count), :] = jnp.where(r == 0, value[:, :128], value[:, 128:])
 
     def turn_back(row, count):
         value = conv(delta2, weights, 1, row, count, back=True)
         value = (adj[flat(row, count), :].astype(F32) + value).astype(BF16)
         back[flat(row, count), :] = value
-        value = half_slope(pre1[flat(row, count), :]) * value.astype(F32)
-        delta1[span(row, count), :] = value.astype(BF16)
-
-    second(inner(f), 6)
+        value = slope1[flat(row, count), :] * value.astype(F32)
+        value = value.astype(BF16)
+        delta1[span(row, count), :] = value
+        delta1_out[flat(row, count), :] = jnp.where(r == 0, value[:, :128], value[:, 128:])
+
+    slope2[flat(inner(f), 6), :] = second(inner(f), 6)
     x2_in(g, 1)
     x2_in(g, 2)
-    advance(x2, mid3, weights, 0, 7 - 2 * f, 4, pre1)
-    second(6, 4)
+    advance(x2, mid3, weights, 0, 7 - 2 * f, 4, slope1)
+    slope2[flat(6, 4), :] = second(6, 4)
     remote(cotangent, adj.at[flat(own, BAND)], 5, adj_sem.at[r], (l, o)).wait_recv()
 
     @pl.when(even | last)
     def _():
         adj_in.wait_recv()
 
-    turn(6 * f, 10)
+    turn(6 * f, 10, slope2[flat(6 * f, 10), :])
     turn_back(7 * f, 9)
 
     x2_in(g, 0)
-    half = pl.ds(pl.multiple_of(r * 128, 128), 128)
     outs = [pltpu.make_async_copy(x2.at[span(0, ROWS)], states_out, out_sem.at[0])]
     outs[-1].start()
-    advance(x2, mid3, weights, 0, 11 * g, 5, pre1)
+    advance(x2, mid3, weights, 0, 11 * g, 5, slope1)
     outs.append(pltpu.make_async_copy(mid3.at[span(0, ROWS)], middle_out, out_sem.at[1]))
     outs[-1].start()
-    second(10 * g, 6)
-    turn(10 * g, 6)
-    outs.append(pltpu.make_async_copy(delta2.at[span(0, ROWS), half], delta2_out, out_sem.at[2]))
-    outs[-1].start()
+    turn(10 * g, 6, second(10 * g, 6))
     turn_back(9 * g, 7)
-    outs.append(pltpu.make_async_copy(delta1.at[span(0, ROWS), half], delta1_out, out_sem.at[3]))
-    outs[-1].start()
 
     value = conv(delta1, weights, 0, own, BAND, back=True)
-    adj_own[...] = (back[flat(own, BAND), :].astype(F32) + value).astype(BF16)
-    outs.append(pltpu.make_async_copy(adj_own, adjoint_out, out_sem.at[4]))
-    outs[-1].start()
+    adjoint_out[...] = (back[flat(own, BAND), :].astype(F32) + value).astype(BF16)
 
     halo.wait_send()
     for here, copies in (
@@ -361,33 +361,21 @@
     scale,
     states, middle, delta1, delta2, adjoint,
     states_out, adjoint_out, grad_out,
-    x, m, d1, d2, adj, wide, grads, sem, out_sem,
+    wide, grads, out_sem, grad_sem,
 ):
     r = lax.axis_index("rows")
-    loads = [
-        pltpu.make_async_copy(middle, m, sem.at[0]),
-        pltpu.make_async_copy(delta2, d2, sem.at[1]),
-        pltpu.make_async_copy(states, x, sem.at[2]),
-        pltpu.make_async_copy(delta1, d1, sem.at[3]),
-        pltpu.make_async_copy(adjoint, adj, sem.at[4]),
-    ]
-    for copy in loads:
+    outs = [
+        pltpu.make_async_copy(states.at[flat(r * BAND, BAND)], states_out, out_sem.at[0]),
+        pltpu.make_async_copy(adjoint, adjoint_out, out_sem.at[1]),
+    ]
+    for copy in outs:
         copy.start()
-    outs = []
     zero = jnp.zeros((W, 384), BF16)
     for layer in range(2):
         wide[layer, pl.ds(0, W), :] = zero
         wide[layer, pl.ds((ROWS + 1) * W, W), :] = zero
     col = lax.broadcasted_iota(jnp.int32, (PX, 128), 0) % W
-    for layer, image, delta, pair in ((1, m, d2, 0), (0, x, d1, 2)):
-        loads[pair].wait()
-        loads[pair + 1].wait()
-        if layer == 0:
-            loads[4].wait()
-            outs.append(pltpu.make_async_copy(x.at[flat(r * BAND, BAND)], states_out, out_sem.at[0]))
-            outs.append(pltpu.make_async_copy(adj, adjoint_out, out_sem.at[1]))
-            for copy in outs[-2:]:
-                copy.start()
+    for layer, image, delta in ((1, middle, delta2), (0, states, delta1)):
         value = delta[...].astype(F32)
         after = jnp.where(col == W - 1, 0.0, pltpu.roll(value, PX - 1, 0))
         before = jnp.where(col == 0, 0.0, pltpu.roll(value, 1, 0))
@@ -395,13 +383,20 @@
         wide[layer, pl.ds(W, PX), 128:256] = delta[...]
         wide[layer, pl.ds(W, PX), 256:384] = before.astype(BF16)
         side = jnp.concatenate([wide[layer, pl.ds((2 - a) * W, PX), :] for a in range(3)], axis=1)
-        terms = lax.dot_general(
-            image[...], side, (((0,), (0,)), ((), ())), preferred_element_type=F32
-        )
-        for tap in range(9):
-            grads[layer, tap] = terms[:, tap * 128 : (tap + 1) * 128] * scale
-        outs.append(pltpu.make_async_copy(grads.at[layer], grad_out.at[layer], out_sem.at[2 + layer]))
-        outs[-1].start()
+        for part, (low, high) in enumerate(((0, 4), (4, 8), (8, 9))):
+            terms = lax.dot_general(
+                image[...], side[:, low * 128 : high * 128], (((0,), (0,)), ((), ())),
+                preferred_element_type=F32,
+            )
+            for tap in range(low, high):
+                grads[layer, tap] = terms[:, (tap - low) * 128 : (tap - low + 1) * 128] * scale
+            taps = pl.ds(low, high - low)
+            outs.append(
+                pltpu.make_async_copy(
+                    grads.at[layer, taps], grad_out.at[layer, taps], grad_sem.at[layer, part]
+                )
+            )
+            outs[-1].start()
     for copy in outs:
         copy.wait()
 
@@ -424,25 +419,25 @@
         states, middle, delta1, delta2, adjoint = pl.pallas_call(
             lambda *refs: sweep_kernel(layers, *refs),
             out_shape=(
-                sds((PX, C), BF16), sds((PX, C), BF16), sds((PX, 128), BF16), sds((PX, 128), BF16),
-                sds((BPX, C), BF16),
+                pltpu.VMEM((PX, C), BF16), pltpu.VMEM((PX, C), BF16),
+                pltpu.VMEM((PX, 128), BF16), pltpu.VMEM((PX, 128), BF16),
+                pltpu.VMEM((BPX, C), BF16),
             ),
             in_specs=[hbm] * 5,
-            out_specs=[hbm] * 5,
+            out_specs=[pl.BlockSpec(memory_space=pltpu.VMEM)] * 5,
             scratch_shapes=[
                 pltpu.VMEM((18, C, C), BF16),
                 image(18), image(18), image(18), image(18), image(18), image(18), image(18),
                 image(16), image(18), image(16), image(18),
                 pltpu.VMEM((PX, C), F32),
                 pltpu.VMEM((PX, C), F32),
-                image(8),
                 pltpu.SemaphoreType.DMA((3,)),
                 pltpu.SemaphoreType.DMA((22,)),
                 pltpu.SemaphoreType.DMA((1,)),
                 pltpu.SemaphoreType.DMA((3,)),
                 pltpu.SemaphoreType.DMA((2, 3)),
                 pltpu.SemaphoreType.DMA((2,)),
-                pltpu.SemaphoreType.DMA((5,)),
+                pltpu.SemaphoreType.DMA((2,)),
             ],
             compiler_params=pltpu.CompilerParams(
                 collective_id=0, has_side_effects=True, vmem_limit_bytes=60 << 20
@@ -452,20 +447,17 @@
         states, adjoint, grads = pl.pallas_call(
             lambda *refs: grad_kernel(scale, *refs),
             out_shape=(sds((BPX, C), BF16), sds((BPX, C), BF16), sds((2, 9, C, 128), F32)),
-            in_specs=[hbm] * 5,
+            in_specs=[pl.BlockSpec(memory_space=pltpu.VMEM)] * 5,
             out_specs=[hbm] * 3,
             scratch_shapes=[
-                image(16), image(16),
-                pltpu.VMEM((PX, 128), BF16), pltpu.VMEM((PX, 128), BF16),
-                image(8),
                 pltpu.VMEM((2, 18 * W, 384), BF16),
                 pltpu.VMEM((2, 9, C, 128), F32),
-                pltpu.SemaphoreType.DMA((5,)),
-                pltpu.SemaphoreType.DMA((4,)),
+                pltpu.SemaphoreType.DMA((2,)),
+                pltpu.SemaphoreType.DMA((2, 3)),
             ],
             compiler_params=pltpu.CompilerParams(vmem_limit_bytes=56 << 20),
             name="weight_grads",
-        )(states, middle, delta1, delta2, adjoint)
+        )(*[pltpu.with_memory_space_constraint(x, pltpu.VMEM) for x in (states, middle, delta1, delta2, adjoint)])
         shape = (1, 1, BAND, W, C)
         return states.reshape(shape), adjoint.reshape(shape), grads
 

time: 32.1 us -> 29.6 us (0.922)
  Pallas kernels: 30.9 us -> 28.7 us
    pallas_call x1, Pallas kernels: 4 us -> 2.34 us  [local(): pl.pallas_call(lambda *refs: grad_kernel(scale, *refs), out_shape=(sds((B...]
    pallas_call x1, Pallas kernels: 26.9 us -> 26.3 us  [local(): pl.pallas_call(lambda *refs: sweep_kernel(layers, *refs), out_shape=(pltp...]
where the time goes in v4:
time: 29.6 us; the launch traced here: 29.5 us
  Pallas kernels  28.7 us (97%)
  between operations  0.8 us (3%)
    pallas_call x1, Pallas kernels, local(): pl.pallas_call(lambda *refs: sweep_kernel(layers, *refs), out_shape=(pltp...  26.3 us
    pallas_call x1, Pallas kernels, local(): pl.pallas_call(lambda *refs: grad_kernel(scale, *refs), out_shape=(sds((B...  2.34 us

profile of v4, /device:TPU:97, one launch (start us, length us, event | category | flops | bytes accessed | tf_op | source)
XLA Modules:
  0.0 29.5 jit_solution(2484346485424112491)
XLA Ops:
  0.6 26.3 %sweeps.1 = (bf16[1024,256]{1,0:T(8,128)(2,1)S(1)}, bf16[1024,256]{1,0:T(8,128)(2,1)S(1)}, bf16[1024,128]{1,0:T(8,128)(2,1)S(1)}, bf16[1024,128]{1,0:T(8,128)(2,1)S(1)}, bf16[512,256]{1,0:T(8,128)(2,1)S(1)}) custom-call(bf16[512,256]{1,0:T(8,128)(2,1)} %bitcast.8, bf16[512,256]{1,0:T(8,128)(2,1)} %bitcast.9, bf16[18,256,256]{2,1,0:T(8,128)(2,1)} %bitcast.7, ...), custom_call_target="tpu_custom_call" | custom-call | tf_op jit(solution)/shard_map/sweeps/pallas_call | solution.py:419
  27.0 2.3 %weight_grads.1 = (bf16[512,256]{1,0:T(8,128)(2,1)}, bf16[512,256]{1,0:T(8,128)(2,1)}, f32[2,9,256,128]{3,2,1,0:T(8,128)}) custom-call(bf16[1024,256]{1,0:T(8,128)(2,1)S(1)} %get-tuple-element.11.refs_0_, bf16[1024,256]{1,0:T(8,128)(2,1)S(1)} %get-tuple-element.12.refs_1_, bf16[1024,128]{1,0:T(8,128)(2,1)S(1)} %get-tuple-element.13.refs_2_, ...), custom_call_target="tpu_custom_call" | custom-call | tf_op jit(solution)/shard_map/weight_grads/pallas_call | solution.py:447

commit v5 on v4

--- a/solution.py
+++ b/solution.py
@@ -16,6 +16,7 @@
 C = 256
 PX = ROWS * W
 BPX = BAND * W
+SPLIT = 4
 
 
 def span(row, count):
@@ -52,6 +53,11 @@
     return shifted[1] + left + right
 
 
+def pieces(row, count):
+    low = count // 2
+    return ((row, low), (row + low, count - low)) if count >= SPLIT else ((row, count),)
+
+
 def sigmoid(value):
     return 1.0 / (1.0 + jnp.exp(-value))
 
@@ -60,13 +66,14 @@
     return 0.5 * s * (1.0 + value * (1.0 - s))
 
 
-def advance(src, dst, weights, layer, row, count, slope=None):
-    value = conv(src, weights, layer, row, count)
-    s = sigmoid(value)
-    state = src[span(row, count), :].astype(F32)
-    dst[span(row, count), :] = (state + 0.5 * value * s).astype(BF16)
-    if slope is not None:
-        slope[flat(row, count), :] = half_slope(value, s)
+def advance(src, dst, weights, layer, start, total, slope=None):
+    for row, count in pieces(start, total):
+        value = conv(src, weights, layer, row, count)
+        s = sigmoid(value)
+        state = src[span(row, count), :].astype(F32)
+        dst[span(row, count), :] = (state + 0.5 * value * s).astype(BF16)
+        if slope is not None:
+            slope[flat(row, count), :] = half_slope(value, s)
 
 
 def sweep_kernel(
@@ -74,7 +81,7 @@
     guess, adj_guess, weights_hbm, net_input, cotangent,
     states_out, middle_out, delta1_out, delta2_out, adjoint_out,
     weights, x0, x1, x2, mid, mid3, end1, end2, adj, delta2, back, delta1, slope1, slope2,
-    load_sem, send_sem, halo_sem, x1_sem, x2_sem, adj_sem, out_sem,
+    load_sem, ready_sem, send_sem, halo_sem, x1_sem, x2_sem, adj_sem, out_sem,
 ):
     l = lax.axis_index("layer")
     r = lax.axis_index("rows")
@@ -101,17 +108,18 @@
         copy.start()
 
     barrier = pltpu.get_barrier_semaphore()
+
+    def greet(here, *devices):
+        @pl.when(here)
+        def _():
+            for device in devices:
+                pl.semaphore_signal(barrier, inc=1, device_id=device, device_id_type=MESH)
+
+    greet(even & takes, (down, o))
+    greet(odd & passes, (up, o))
     pl.semaphore_signal(barrier, inc=1, device_id=(l, o), device_id_type=MESH)
-
-    @pl.when(jnp.logical_not(first))
-    def _():
-        pl.semaphore_signal(barrier, inc=1, device_id=(down, r), device_id_type=MESH)
-        pl.semaphore_signal(barrier, inc=1, device_id=(down, o), device_id_type=MESH)
-
-    @pl.when(jnp.logical_not(last))
-    def _():
-        pl.semaphore_signal(barrier, inc=1, device_id=(up, r), device_id_type=MESH)
-        pl.semaphore_signal(barrier, inc=1, device_id=(up, o), device_id_type=MESH)
+    greet(even, (up, r), (up, o))
+    greet(odd, (down, r), (down, o))
 
     zero = jnp.zeros((W, C), BF16)
     for buf in (x0, x1, x2, mid, mid3, delta2, delta1):
@@ -124,7 +132,11 @@
 
     @pl.when(jnp.logical_not(first | last))
     def _():
-        pl.semaphore_wait(barrier, 5)
+        pl.semaphore_wait(barrier, 4)
+
+    @pl.when(even & takes)
+    def _():
+        pl.semaphore_signal(ready_sem, inc=1, device_id=(down, o), device_id_type=MESH)
 
     def remote(src, dst, send, recv, device):
         return pltpu.make_async_remote_copy(
@@ -175,38 +187,45 @@
     def _():
         adj_same.start()
 
-    def sweep(src, dst, band, rest, edge_in, send):
-        advance(src, mid, weights, 0, 9 * band, 7)
-        rest()
-        advance(mid, dst, weights, 1, inner(band), 6)
-        send(False)
-        edge_in.wait_recv()
-        advance(src, mid, weights, 0, 7, 2)
-        advance(mid, dst, weights, 1, edge(band), 2)
-        send(True)
-
-    e1_inner = ship(end1, x1, inner(r), 6, 9, x1_sem.at[0], (up, t))
+    e1_inner = [
+        ship(end1, x1, rows, 3, send, x1_sem.at[0], (up, t))
+        for rows, send in ((13 * r, 9), (3 + 7 * r, 22))
+    ]
     e1_edge = ship(end1, x1, edge(r), 2, 10, x1_sem.at[0], (up, t))
     e1_cross = ship(end1, x1, edge(r), 2, 11, x1_sem.at[1], (up, 1 - t))
     e1_rest = ship(end1, x1, inner(r), 6, 12, x1_sem.at[2], (up, o))
 
-    def send1(late):
-        @pl.when(passes)
-        def _():
-            if late:
-                e1_cross.start()
-                e1_edge.start()
-            else:
-                e1_inner.start()
-
-        if late:
-
-            @pl.when(even)
-            def _():
-                e1_rest.start()
-
     loads[1].wait()
-    sweep(x0, end1, r, loads[2].wait, halo_in, send1)
+    advance(x0, mid, weights, 0, 12 * r, 4)
+    loads[2].wait()
+    advance(mid, end1, weights, 1, 13 * r, 3)
+
+    @pl.when(passes)
+    def _():
+        e1_inner[0].start()
+
+    advance(x0, mid, weights, 0, 4 + 5 * r, 3)
+    advance(mid, end1, weights, 1, 3 + 7 * r, 3)
+
+    @pl.when(passes)
+    def _():
+        e1_inner[1].start()
+
+    halo_in.wait_recv()
+    advance(x0, mid, weights, 0, 7, 2)
+    advance(mid, end1, weights, 1, edge(r), 2)
+
+    @pl.when(even)
+    def _():
+        e1_cross.start()
+        e1_edge.start()
+        e1_rest.start()
+
+    @pl.when(odd & passes)
+    def _():
+        e1_edge.start()
+        pl.semaphore_wait(ready_sem, 1)
+        e1_cross.start()
 
     @pl.when(last)
     def _():
@@ -224,14 +243,6 @@
         ship(end2, x2, rows(s), count, 16 + part, x2_sem.at[s, part], (up, r))
         for part, (rows, count) in enumerate(parts)
     ]
-
-    def send2(late):
-        which = slice(2, 3) if late else slice(0, 2)
-
-        @pl.when(passes)
-        def _():
-            for copy in e2[which]:
-                copy.start()
 
     q = 1 - s
     x1_own = ship(end1, x1, s * BAND, BAND, 9, x1_sem.at[0], (l, o))
@@ -256,19 +267,39 @@
         x1_edge.wait_recv()
         advance(x1, mid, weights, 0, 7 * s, 9)
         advance(mid, end2, weights, 1, s * BAND, BAND)
+
+        @pl.when(first)
+        def _():
+            nets2[2].start()
+            nets2[1].start()
+
         for part in (2, 1, 0):
             e2_same[part].start()
             e2[part].start()
 
         @pl.when(first)
         def _():
-            for copy in nets2[::-1]:
-                copy.start()
+            nets2[0].start()
 
     @pl.when(odd)
     def _():
         x1_own.wait_recv()
-        sweep(x1, end2, s, lambda: None, x1_edge, send2)
+        advance(x1, mid, weights, 0, 9 * s, 7)
+        advance(mid, end2, weights, 1, inner(s), 6)
+
+        @pl.when(passes)
+        def _():
+            e2[0].start()
+            e2[1].start()
+
+        x1_edge.wait_recv()
+        advance(x1, mid, weights, 0, 7, 2)
+        advance(mid, end2, weights, 1, edge(s), 2)
+
+        @pl.when(passes)
+        def _():
+            e2[2].start()
+
         pass_adjoint(jnp.logical_not(distant))
         x1_rest.wait_recv()
 
@@ -278,11 +309,14 @@
             advance(mid, end2, weights, 1, 4 + 4 * q, 4)
             for copy in e2_other[1:]:
                 copy.start()
+
+        pass_adjoint(distant)
+
+        @pl.when(passes)
+        def _():
             advance(x1, mid, weights, 0, 13 * q, 3)
             advance(mid, end2, weights, 1, far(q), 4)
             e2_other[0].start()
-
-        pass_adjoint(distant)
 
     x2_in = lambda band, part: ship(
         end2, x2, parts[part][0](band), parts[part][1], 13, x2_sem.at[band, part], (l, o)
@@ -293,29 +327,34 @@
         x2_in(f, part)
     advance(x2, mid3, weights, 0, 9 * f, 7, slope1)
 
-    def second(row, count):
-        value = conv(mid3, weights, 1, row, count)
-        return half_slope(value, sigmoid(value))
+    def second(start, total, then=None):
+        for row, count in pieces(start, total):
+            value = conv(mid3, weights, 1, row, count)
+            value = half_slope(value, sigmoid(value))
+            if then is None:
+                slope2[flat(row, count), :] = value
+            else:
+                then(row, count, value)
 
     def turn(row, count, slope):
         value = (slope * adj[flat(row, count), :].astype(F32)).astype(BF16)
         delta2[span(row, count), :] = value
         delta2_out[flat(row, count), :] = jnp.where(r == 0, value[:, :128], value[:, 128:])
 
-    def turn_back(row, count):
-        value = conv(delta2, weights, 1, row, count, back=True)
-        value = (adj[flat(row, count), :].astype(F32) + value).astype(BF16)
-        back[flat(row, count), :] = value
-        value = slope1[flat(row, count), :] * value.astype(F32)
-        value = value.astype(BF16)
-        delta1[span(row, count), :] = value
-        delta1_out[flat(row, count), :] = jnp.where(r == 0, value[:, :128], value[:, 128:])
-
-    slope2[flat(inner(f), 6), :] = second(inner(f), 6)
+    def turn_back(start, total):
+        for row, count in pieces(start, total):
+            value = conv(delta2, weights, 1, row, count, back=True)
+            value = (adj[flat(row, count), :].astype(F32) + value).astype(BF16)
+            back[flat(row, count), :] = value
+            value = (slope1[flat(row, count), :] * value.astype(F32)).astype(BF16)
+            delta1[span(row, count), :] = value
+            delta1_out[flat(row, count), :] = jnp.where(r == 0, value[:, :128], value[:, 128:])
+
+    second(inner(f), 6)
     x2_in(g, 1)
     x2_in(g, 2)
     advance(x2, mid3, weights, 0, 7 - 2 * f, 4, slope1)
-    slope2[flat(6, 4), :] = second(6, 4)
+    second(6, 4)
     remote(cotangent, adj.at[flat(own, BAND)], 5, adj_sem.at[r], (l, o)).wait_recv()
 
     @pl.when(even | last)
@@ -331,11 +370,13 @@
     advance(x2, mid3, weights, 0, 11 * g, 5, slope1)
     outs.append(pltpu.make_async_copy(mid3.at[span(0, ROWS)], middle_out, out_sem.at[1]))
     outs[-1].start()
-    turn(10 * g, 6, second(10 * g, 6))
+    second(10 * g, 6, turn)
     turn_back(9 * g, 7)
 
-    value = conv(delta1, weights, 0, own, BAND, back=True)
-    adjoint_out[...] = (back[flat(own, BAND), :].astype(F32) + value).astype(BF16)
+    for row, count in pieces(own, BAND):
+        value = conv(delta1, weights, 0, row, count, back=True)
+        at = flat(row - own, count)
+        adjoint_out[at, :] = (back[flat(row, count), :].astype(F32) + value).astype(BF16)
 
     halo.wait_send()
     for here, copies in (
@@ -344,7 +385,7 @@
         (takes, [adj_cross]),
         (odd, [adj_same]),
         (odd & passes, [adj_on] + e2_other),
-        (passes, [e1_inner, e1_edge, e1_cross] + e2),
+        (passes, e1_inner + [e1_edge, e1_cross] + e2),
         (even, [e1_rest] + e2_same),
     ):
 
@@ -432,7 +473,8 @@
                 pltpu.VMEM((PX, C), F32),
                 pltpu.VMEM((PX, C), F32),
                 pltpu.SemaphoreType.DMA((3,)),
-                pltpu.SemaphoreType.DMA((22,)),
+                pltpu.SemaphoreType.REGULAR,
+                pltpu.SemaphoreType.DMA((23,)),
                 pltpu.SemaphoreType.DMA((1,)),
                 pltpu.SemaphoreType.DMA((3,)),
                 pltpu.SemaphoreType.DMA((2, 3)),

time: 29.6 us -> 28.3 us (0.956)
  Pallas kernels: 28.7 us -> 27.4 us
    pallas_call x1, Pallas kernels: 26.3 us -> 25 us  [local(): pl.pallas_call(lambda *refs: sweep_kernel(layers, *refs), out_shape=(pltp...]
where the time goes in v5:
time: 28.3 us; the launch traced here: 28.2 us
  Pallas kernels  27.4 us (97%)
  between operations  0.8 us (3%)
    pallas_call x1, Pallas kernels, local(): pl.pallas_call(lambda *refs: sweep_kernel(layers, *refs), out_shape=(pltp...  25 us
    pallas_call x1, Pallas kernels, local(): pl.pallas_call(lambda *refs: grad_kernel(scale, *refs), out_shape=(sds((B...  2.34 us

profile of v5, /device:TPU:97, one launch (start us, length us, event | category | flops | bytes accessed | tf_op | source)
XLA Modules:
  0.0 28.2 jit_solution(5430112007386453160)
XLA Ops:
  0.6 25.0 %sweeps.1 = (bf16[1024,256]{1,0:T(8,128)(2,1)S(1)}, bf16[1024,256]{1,0:T(8,128)(2,1)S(1)}, bf16[1024,128]{1,0:T(8,128)(2,1)S(1)}, bf16[1024,128]{1,0:T(8,128)(2,1)S(1)}, bf16[512,256]{1,0:T(8,128)(2,1)S(1)}) custom-call(bf16[512,256]{1,0:T(8,128)(2,1)} %bitcast.8, bf16[512,256]{1,0:T(8,128)(2,1)} %bitcast.9, bf16[18,256,256]{2,1,0:T(8,128)(2,1)} %bitcast.7, ...), custom_call_target="tpu_custom_call" | custom-call | tf_op jit(solution)/shard_map/sweeps/pallas_call | solution.py:460
  25.6 2.3 %weight_grads.1 = (bf16[512,256]{1,0:T(8,128)(2,1)}, bf16[512,256]{1,0:T(8,128)(2,1)}, f32[2,9,256,128]{3,2,1,0:T(8,128)}) custom-call(bf16[1024,256]{1,0:T(8,128)(2,1)S(1)} %get-tuple-element.11.refs_0_, bf16[1024,256]{1,0:T(8,128)(2,1)S(1)} %get-tuple-element.12.refs_1_, bf16[1024,128]{1,0:T(8,128)(2,1)S(1)} %get-tuple-element.13.refs_2_, ...), custom_call_target="tpu_custom_call" | custom-call | tf_op jit(solution)/shard_map/weight_grads/pallas_call | solution.py:489

commit v6 on v5

--- a/solution.py
+++ b/solution.py
@@ -193,7 +193,10 @@
     ]
     e1_edge = ship(end1, x1, edge(r), 2, 10, x1_sem.at[0], (up, t))
     e1_cross = ship(end1, x1, edge(r), 2, 11, x1_sem.at[1], (up, 1 - t))
-    e1_rest = ship(end1, x1, inner(r), 6, 12, x1_sem.at[2], (up, o))
+    e1_rest = [
+        ship(end1, x1, 2 + 8 * r, 4, 12, x1_sem.at[2], (up, o)),
+        ship(end1, x1, 14 * r, 2, 23, x1_sem.at[3], (up, o)),
+    ]
 
     loads[1].wait()
     advance(x0, mid, weights, 0, 12 * r, 4)
@@ -219,7 +222,8 @@
     def _():
         e1_cross.start()
         e1_edge.start()
-        e1_rest.start()
+        for copy in e1_rest:
+            copy.start()
 
     @pl.when(odd & passes)
     def _():
@@ -247,7 +251,10 @@
     q = 1 - s
     x1_own = ship(end1, x1, s * BAND, BAND, 9, x1_sem.at[0], (l, o))
     x1_edge = ship(end1, x1, edge(q), 2, 11, x1_sem.at[1], (l, o))
-    x1_rest = ship(end1, x1, inner(q), 6, 12, x1_sem.at[2], (l, o))
+    x1_rest = [
+        ship(end1, x1, 2 + 8 * q, 4, 12, x1_sem.at[2], (l, o)),
+        ship(end1, x1, 14 * q, 2, 23, x1_sem.at[3], (l, o)),
+    ]
     e2_other = [
         ship(end2, x2, rows(q), count, 19 + part, x2_sem.at[q, part], (up, o))
         for part, (rows, count) in enumerate(parts)
@@ -273,9 +280,8 @@
             nets2[2].start()
             nets2[1].start()
 
-        for part in (2, 1, 0):
-            e2_same[part].start()
-            e2[part].start()
+        for copy in (e2[2], e2[1], e2_same[2], e2_same[1], e2_same[0], e2[0]):
+            copy.start()
 
         @pl.when(first)
         def _():
@@ -301,7 +307,7 @@
             e2[2].start()
 
         pass_adjoint(jnp.logical_not(distant))
-        x1_rest.wait_recv()
+        x1_rest[0].wait_recv()
 
         @pl.when(passes)
         def _():
@@ -311,6 +317,7 @@
                 copy.start()
 
         pass_adjoint(distant)
+        x1_rest[1].wait_recv()
 
         @pl.when(passes)
         def _():
@@ -386,7 +393,7 @@
         (odd, [adj_same]),
         (odd & passes, [adj_on] + e2_other),
         (passes, e1_inner + [e1_edge, e1_cross] + e2),
-        (even, [e1_rest] + e2_same),
+        (even, e1_rest + e2_same),
     ):
 
         @pl.when(here)
@@ -474,9 +481,9 @@
                 pltpu.VMEM((PX, C), F32),
                 pltpu.SemaphoreType.DMA((3,)),
                 pltpu.SemaphoreType.REGULAR,
-                pltpu.SemaphoreType.DMA((23,)),
+                pltpu.SemaphoreType.DMA((24,)),
                 pltpu.SemaphoreType.DMA((1,)),
-                pltpu.SemaphoreType.DMA((3,)),
+                pltpu.SemaphoreType.DMA((4,)),
                 pltpu.SemaphoreType.DMA((2, 3)),
                 pltpu.SemaphoreType.DMA((2,)),
                 pltpu.SemaphoreType.DMA((2,)),

time: 28.3 us -> 28.3 us (level)
  no operation moved by 1% of the time
where the time goes in v6:
time: 28.3 us; the launch traced here: 28.2 us
  Pallas kernels  27.4 us (97%)
  between operations  0.8 us (3%)
    pallas_call x1, Pallas kernels, local(): pl.pallas_call(lambda *refs: sweep_kernel(layers, *refs), out_shape=(pltp...  25 us
    pallas_call x1, Pallas kernels, local(): pl.pallas_call(lambda *refs: grad_kernel(scale, *refs), out_shape=(sds((B...  2.34 us

profile of v6, /device:TPU:97, one launch (start us, length us, event | category | flops | bytes accessed | tf_op | source)
XLA Modules:
  0.0 28.2 jit_solution(17091437076940895233)
XLA Ops:
  0.6 25.0 %sweeps.1 = (bf16[1024,256]{1,0:T(8,128)(2,1)S(1)}, bf16[1024,256]{1,0:T(8,128)(2,1)S(1)}, bf16[1024,128]{1,0:T(8,128)(2,1)S(1)}, bf16[1024,128]{1,0:T(8,128)(2,1)S(1)}, bf16[512,256]{1,0:T(8,128)(2,1)S(1)}) custom-call(bf16[512,256]{1,0:T(8,128)(2,1)} %bitcast.8, bf16[512,256]{1,0:T(8,128)(2,1)} %bitcast.9, bf16[18,256,256]{2,1,0:T(8,128)(2,1)} %bitcast.7, ...), custom_call_target="tpu_custom_call" | custom-call | tf_op jit(solution)/shard_map/sweeps/pallas_call | solution.py:467
  25.7 2.3 %weight_grads.1 = (bf16[512,256]{1,0:T(8,128)(2,1)}, bf16[512,256]{1,0:T(8,128)(2,1)}, f32[2,9,256,128]{3,2,1,0:T(8,128)}) custom-call(bf16[1024,256]{1,0:T(8,128)(2,1)S(1)} %get-tuple-element.11.refs_0_, bf16[1024,256]{1,0:T(8,128)(2,1)S(1)} %get-tuple-element.12.refs_1_, bf16[1024,128]{1,0:T(8,128)(2,1)S(1)} %get-tuple-element.13.refs_2_, ...), custom_call_target="tpu_custom_call" | custom-call | tf_op jit(solution)/shard_map/weight_grads/pallas_call | solution.py:496
